TPU v7x, 256 devices: a whole 4x4x8 slice. The times are simulated.
256 devices in a mesh: seq: 64 (over x, z, core), rep: 4 (over y).
Axes of the slice: x: 4, y: 4, z: 8, core: 2. Of those that a mesh axis runs over, the one named last changes fastest.
Arguments:
- query_in: bfloat16 [4, 8192, 1024], P('rep', 'seq'), may hold values from -120 to 120
- key_in: bfloat16 [4, 8192, 1024], P('rep', 'seq'), may hold values from -4 to 4
- value_in: bfloat16 [4, 8192, 1024], P('rep', 'seq'), may hold values from -6 to 6
- out_weight: bfloat16 [1024, 2048], replicated, may hold values from -0.1875 to 0.1875
- grad_out: bfloat16 [4, 8192, 2048], P('rep', 'seq'), may hold values from -6 to 6
- pattern: int32 [128, 8], replicated, may hold values from 0 to 127, as said below
Outputs:
- mixed_out: bfloat16 [4, 8192, 2048], P('rep', 'seq')
- query_grad: bfloat16 [4, 8192, 1024], P('rep', 'seq')
- key_grad: bfloat16 [4, 8192, 1024], P('rep', 'seq')
- value_grad: bfloat16 [4, 8192, 1024], P('rep', 'seq')
- weight_grad: float32 [1024, 2048], P('seq')
Inputs may be any that keep to these rules, and one draw needn't show every extreme that they name: `pattern`: row b names blocks b - 1, b and b + 1 modulo 128 in columns 0 to 2; columns 3 and 4 hold the same two blocks in every row; the other columns may name any block.
All inputs are finite; a program needn't handle non-finite values.
Results may differ from a plain program's by a relative error of at most 0.0095.
Values may be sent and summed in bfloat16 or wider, within the bound.
A program may use at most 128 MiB of HBM per device.

v0:
```python
import math

import jax
import jax.numpy as jnp
from jax import lax
from jax.sharding import PartitionSpec as P

HD = 128
BLK = 64


def in_one_piece(arrays, axis, split_dim, concat_dim, along):
    widths = [a.shape[along] for a in arrays]
    both = jnp.concatenate(arrays, axis=along)
    result = lax.all_to_all(both, axis, split_axis=split_dim, concat_axis=concat_dim, tiled=True)
    return tuple(jnp.split(result, [sum(widths[:k]) for k in range(1, len(widths))], axis=along))


def sent_to_all(value, axis):
    copies = jnp.broadcast_to(value, (lax.axis_size(axis), *value.shape))
    return lax.all_to_all(copies, axis, split_axis=0, concat_axis=0, tiled=True)


def taken_together(value, axis):
    return sent_to_all(value, axis).astype(jnp.float32).sum(axis=0)


def local(query_in, key_in, value_in, out_weight, grad_out, pattern):
    seq_count = lax.axis_size("seq")
    rep_count = lax.axis_size("rep")
    tokens_here = query_in.shape[1]
    width = query_in.shape[2]
    head_size = HD
    head_count = width // head_size
    groups = max(seq_count // head_count, 1)
    per_device = max(head_count // seq_count, 1)
    head_groups = head_count // per_device
    local_blocks = tokens_here // BLK
    group_rows = BLK // groups
    all_blocks = seq_count * local_blocks
    columns = per_device * head_size
    span = pattern.shape[1]
    block_run = math.gcd(all_blocks, 32)
    run_count = all_blocks // block_run
    scale = 1.0 / math.sqrt(head_size)

    def to_heads(source):
        shaped = source.reshape(local_blocks, groups, group_rows, head_groups, columns)
        return shaped.transpose(3, 1, 0, 2, 4).reshape(
            seq_count, local_blocks * group_rows, columns
        )

    def to_tokens(source):
        shaped = source.reshape(head_groups, groups, local_blocks, group_rows, columns)
        return shaped.transpose(2, 1, 3, 0, 4).reshape(tokens_here, width)

    query_local = query_in[0]
    key_local = key_in[0]
    value_local = value_in[0]
    grad_local = grad_out[0]

    def spread(source):
        grouped = source.reshape(tokens_here, head_groups, columns).transpose(1, 0, 2)
        copies = jnp.broadcast_to(grouped[:, None], (head_groups, groups, tokens_here, columns))
        return copies.reshape(seq_count, tokens_here, columns)

    query_heads, key_all, value_all = in_one_piece(
        (to_heads(query_local), spread(key_local), spread(value_local)), "seq", 0, 0, 1
    )
    attended_grad = lax.dot_general(
        grad_local, out_weight, (((1,), (1,)), ((), ())), preferred_element_type=jnp.float32
    ).astype(jnp.bfloat16)
    grad_heads = lax.all_to_all(
        to_heads(attended_grad), "seq", split_axis=0, concat_axis=0, tiled=True
    )
    key_blocks = key_all.reshape(all_blocks, BLK, per_device, head_size)
    value_blocks = value_all.reshape(all_blocks, BLK, per_device, head_size)
    query_runs = query_heads.reshape(run_count, block_run, group_rows, per_device, head_size)
    grad_runs = grad_heads.reshape(run_count, block_run, group_rows, per_device, head_size)
    pattern_runs = pattern.reshape(run_count, block_run, span)

    def attend_step(carry, items):
        key_acc, value_acc = carry
        query_run, grad_run, pattern_run = items
        key_gathered = key_blocks[pattern_run].reshape(block_run, span * BLK, per_device, head_size)
        value_gathered = value_blocks[pattern_run].reshape(
            block_run, span * BLK, per_device, head_size
        )
        scores = (
            jnp.einsum(
                "crhd,ckhd->chrk", query_run, key_gathered, preferred_element_type=jnp.float32
            )
            * scale
        )
        shifted = scores - jnp.max(scores, axis=-1, keepdims=True)
        weights = jnp.exp(shifted)
        probs = weights / jnp.sum(weights, axis=-1, keepdims=True)
        probs_low = probs.astype(jnp.bfloat16)
        result = jnp.einsum(
            "chrk,ckhd->crhd", probs_low, value_gathered, preferred_element_type=jnp.float32
        ).astype(jnp.bfloat16)
        prob_grad = jnp.einsum(
            "crhd,ckhd->chrk", grad_run, value_gathered, preferred_element_type=jnp.float32
        )
        delta = jnp.sum(probs * prob_grad, axis=-1, keepdims=True)
        score_grad = (probs * (prob_grad - delta)).astype(jnp.bfloat16)
        query_part = (
            jnp.einsum(
                "chrk,ckhd->crhd", score_grad, key_gathered, preferred_element_type=jnp.float32
            )
            * scale
        ).astype(jnp.bfloat16)
        key_contrib = (
            jnp.einsum("chrk,crhd->ckhd", score_grad, query_run, preferred_element_type=jnp.float32)
            * scale
        )
        value_contrib = jnp.einsum(
            "chrk,crhd->ckhd", probs_low, grad_run, preferred_element_type=jnp.float32
        )
        key_acc = key_acc.at[pattern_run].add(
            key_contrib.reshape(block_run, span, BLK, per_device, head_size)
        )
        value_acc = value_acc.at[pattern_run].add(
            value_contrib.reshape(block_run, span, BLK, per_device, head_size)
        )
        return ((key_acc, value_acc), (result, query_part))

    zero_grads = jnp.zeros((all_blocks, BLK, per_device, head_size), jnp.float32)
    (key_acc, value_acc), (out_heads, query_parts) = lax.scan(
        attend_step, (zero_grads, zero_grads), (query_runs, grad_runs, pattern_runs)
    )
    out_send = out_heads.reshape(seq_count, local_blocks * group_rows, columns)
    attended = to_tokens(lax.all_to_all(out_send, "seq", split_axis=0, concat_axis=0, tiled=True))
    mixed_out = jnp.dot(attended, out_weight, preferred_element_type=jnp.float32).astype(
        jnp.bfloat16
    )
    norm_factor = 1.0 / math.sqrt(rep_count * seq_count * tokens_here)
    weight_shard = lax.psum_scatter(
        lax.dot_general(
            attended, grad_local, (((0,), (0,)), ((), ())), preferred_element_type=jnp.float32
        ),
        "seq",
        scatter_dimension=0,
        tiled=True,
    )
    weight_grad = (
        taken_together(weight_shard.astype(jnp.bfloat16), "rep").astype(jnp.float32) * norm_factor
    )
    query_send = query_parts.reshape(seq_count, local_blocks * group_rows, columns)
    key_send = key_acc.astype(jnp.bfloat16).reshape(seq_count, tokens_here, columns)
    value_send = value_acc.astype(jnp.bfloat16).reshape(seq_count, tokens_here, columns)
    query_back, key_back, value_back = in_one_piece(
        (query_send, key_send, value_send), "seq", 0, 0, 1
    )

    def fold_groups(source):
        summed = jnp.sum(
            source.reshape(head_groups, groups, tokens_here, columns).astype(jnp.float32), axis=1
        )
        return summed.astype(jnp.bfloat16).transpose(1, 0, 2).reshape(tokens_here, width)

    query_grad = to_tokens(query_back)
    key_grad = fold_groups(key_back)
    value_grad = fold_groups(value_back)
    return (mixed_out[None], query_grad[None], key_grad[None], value_grad[None], weight_grad)


def solution(mesh):
    placed = (
        P("rep", "seq", None),
        P("rep", "seq", None),
        P("rep", "seq", None),
        P(),
        P("rep", "seq", None),
        P(),
    )
    return jax.shard_map(
        local,
        mesh=mesh,
        in_specs=placed,
        out_specs=(
            P("rep", "seq", None),
            P("rep", "seq", None),
            P("rep", "seq", None),
            P("rep", "seq", None),
            P("seq", None),
        ),
        check_vma=False,
    )
```

profile of v0, /device:TPU:2, one launch (start us, length us, event | category | flops | bytes accessed | tf_op | source)
XLA Modules:
  0.0 867.1 jit_solution(5480892524817071514)
XLA Ops:
  13.6 12.2 %all-to-all-start = ((bf16[64,272,128]{2,1,0:T(8,128)(2,1)}), bf16[64,272,128]{2,1,0:T(8,128)(2,1)}, u32[]{:S(2)}, u32[]{:S(2)}) async-start(bf16[64,272,128]{2,1,0:T(8,128)(2,1)} %pad_maximum_fusion), calls=%async_computation | async-start | bytes 8912896 | tf_op jit(solution)/shard_map/all_to_all | solution.py:15
  30.3 95.9 %all-to-all-done = bf16[64,272,128]{2,1,0:T(8,128)(2,1)} async-done(((bf16[64,272,128]{2,1,0:T(8,128)(2,1)}), bf16[64,272,128]{2,1,0:T(8,128)(2,1)}, u32[]{:S(2)}, u32[]{:S(2)}) %all-to-all-start) | async-done | bytes 4456480 | tf_op jit(solution)/shard_map/all_to_all | solution.py:15
  126.2 6.9 all-to-all-start.1
  139.2 5.4 all-to-all-done.1
  149.6 502.3 %while.16 = (s32[]{:T(128)}, f32[128,64,1,128]{3,1,0,2:T(8,128)}, f32[128,64,1,128]{3,1,0,2:T(8,128)}, bf16[4,32,8,1,128]{4,2,1,3,0:T(8,128)(2,1)}, bf16[4,32,8,...) while((s32[]{:T(128)}, f32[128,64,1,128]{3,1,0,2:T(8,128)}, ...), condition=%wide.region_6.7_spmd, body=%wide.region_0.6_spmd.sunk | while | flops 209553408 | bytes 174755088 | solution.py:129
  168.1 5.3 convolution_bitcast_fusion.2
  173.5 9.0 %copy.90 = f32[32,512,1,128]{3,1,0,2:T(8,128)} copy(f32[32,512,1,128]{1,3,0,2:T(8,128)} %convolution_bitcast_fusion.2) | data formatting | bytes 16777216 | tf_op jit(solution)/shard_map/while/body/eval_jaxpr/chrk,crhd->ckhd/transpose | solution.py:117
  182.4 39.2 %scatter_fusion.1 = f32[128,64,128]{2,1,0:T(8,128)} fusion(f32[128,64,128]{2,1,0:T(8,128)} %bitcast.177, s32[256]{0:T(256)S(1)} %reshape.261, f32[256,64,128]{2,1,0:T(8,128)} %bitcast.176), kind=kCustom, calls=%fused_computation.3.clone.1 | custom fusion | flops 2097152 | bytes 25166848 | tf_op jit(solution)/shard_map/while/body/eval_jaxpr/scatter-add | solution.py:123
  221.6 5.3 multiply_bitcast_fusion.2
  227.0 9.0 %copy.89 = f32[32,512,1,128]{3,1,0,2:T(8,128)} copy(f32[32,512,1,128]{1,3,0,2:T(8,128)} %multiply_bitcast_fusion.2) | data formatting | bytes 16777216 | tf_op jit(solution)/shard_map/while/body/eval_jaxpr/mul | solution.py:114
  235.9 39.1 %scatter_fusion = f32[128,64,128]{2,1,0:T(8,128)} fusion(f32[128,64,128]{2,1,0:T(8,128)} %bitcast.179, s32[256]{0:T(256)S(1)} %reshape.261, f32[256,64,128]{2,1,0:T(8,128)} %bitcast.175), kind=kCustom, calls=%fused_computation.2.clone.1 | custom fusion | flops 2097152 | bytes 25166848 | tf_op jit(solution)/shard_map/while/body/eval_jaxpr/scatter-add | solution.py:120
  293.6 5.3 convolution_bitcast_fusion.2
  299.0 9.0 %copy.90 = f32[32,512,1,128]{3,1,0,2:T(8,128)} copy(f32[32,512,1,128]{1,3,0,2:T(8,128)} %convolution_bitcast_fusion.2) | data formatting | bytes 16777216 | tf_op jit(solution)/shard_map/while/body/eval_jaxpr/chrk,crhd->ckhd/transpose | solution.py:117
  307.9 39.2 %scatter_fusion.1 = f32[128,64,128]{2,1,0:T(8,128)} fusion(f32[128,64,128]{2,1,0:T(8,128)} %bitcast.177, s32[256]{0:T(256)S(1)} %reshape.261, f32[256,64,128]{2,1,0:T(8,128)} %bitcast.176), kind=kCustom, calls=%fused_computation.3.clone.1 | custom fusion | flops 2097152 | bytes 25166848 | tf_op jit(solution)/shard_map/while/body/eval_jaxpr/scatter-add | solution.py:123
  347.1 5.3 multiply_bitcast_fusion.2
  352.5 9.0 %copy.89 = f32[32,512,1,128]{3,1,0,2:T(8,128)} copy(f32[32,512,1,128]{1,3,0,2:T(8,128)} %multiply_bitcast_fusion.2) | data formatting | bytes 16777216 | tf_op jit(solution)/shard_map/while/body/eval_jaxpr/mul | solution.py:114
  361.4 39.3 %scatter_fusion = f32[128,64,128]{2,1,0:T(8,128)} fusion(f32[128,64,128]{2,1,0:T(8,128)} %bitcast.179, s32[256]{0:T(256)S(1)} %reshape.261, f32[256,64,128]{2,1,0:T(8,128)} %bitcast.175), kind=kCustom, calls=%fused_computation.2.clone.1 | custom fusion | flops 2097152 | bytes 25166848 | tf_op jit(solution)/shard_map/while/body/eval_jaxpr/scatter-add | solution.py:120
  419.3 5.3 convolution_bitcast_fusion.2
  424.7 9.0 %copy.90 = f32[32,512,1,128]{3,1,0,2:T(8,128)} copy(f32[32,512,1,128]{1,3,0,2:T(8,128)} %convolution_bitcast_fusion.2) | data formatting | bytes 16777216 | tf_op jit(solution)/shard_map/while/body/eval_jaxpr/chrk,crhd->ckhd/transpose | solution.py:117
  433.6 39.2 %scatter_fusion.1 = f32[128,64,128]{2,1,0:T(8,128)} fusion(f32[128,64,128]{2,1,0:T(8,128)} %bitcast.177, s32[256]{0:T(256)S(1)} %reshape.261, f32[256,64,128]{2,1,0:T(8,128)} %bitcast.176), kind=kCustom, calls=%fused_computation.3.clone.1 | custom fusion | flops 2097152 | bytes 25166848 | tf_op jit(solution)/shard_map/while/body/eval_jaxpr/scatter-add | solution.py:123
  472.8 5.3 multiply_bitcast_fusion.2
  478.2 9.0 %copy.89 = f32[32,512,1,128]{3,1,0,2:T(8,128)} copy(f32[32,512,1,128]{1,3,0,2:T(8,128)} %multiply_bitcast_fusion.2) | data formatting | bytes 16777216 | tf_op jit(solution)/shard_map/while/body/eval_jaxpr/mul | solution.py:114
  487.1 39.2 %scatter_fusion = f32[128,64,128]{2,1,0:T(8,128)} fusion(f32[128,64,128]{2,1,0:T(8,128)} %bitcast.179, s32[256]{0:T(256)S(1)} %reshape.261, f32[256,64,128]{2,1,0:T(8,128)} %bitcast.175), kind=kCustom, calls=%fused_computation.2.clone.1 | custom fusion | flops 2097152 | bytes 25166848 | tf_op jit(solution)/shard_map/while/body/eval_jaxpr/scatter-add | solution.py:120
  544.9 5.3 convolution_bitcast_fusion.2
  550.2 9.0 %copy.90 = f32[32,512,1,128]{3,1,0,2:T(8,128)} copy(f32[32,512,1,128]{1,3,0,2:T(8,128)} %convolution_bitcast_fusion.2) | data formatting | bytes 16777216 | tf_op jit(solution)/shard_map/while/body/eval_jaxpr/chrk,crhd->ckhd/transpose | solution.py:117
  559.2 39.2 %scatter_fusion.1 = f32[128,64,128]{2,1,0:T(8,128)} fusion(f32[128,64,128]{2,1,0:T(8,128)} %bitcast.177, s32[256]{0:T(256)S(1)} %reshape.261, f32[256,64,128]{2,1,0:T(8,128)} %bitcast.176), kind=kCustom, calls=%fused_computation.3.clone.1 | custom fusion | flops 2097152 | bytes 25166848 | tf_op jit(solution)/shard_map/while/body/eval_jaxpr/scatter-add | solution.py:123
  598.4 5.3 multiply_bitcast_fusion.2
  603.7 9.0 %copy.89 = f32[32,512,1,128]{3,1,0,2:T(8,128)} copy(f32[32,512,1,128]{1,3,0,2:T(8,128)} %multiply_bitcast_fusion.2) | data formatting | bytes 16777216 | tf_op jit(solution)/shard_map/while/body/eval_jaxpr/mul | solution.py:114
  612.7 39.2 %scatter_fusion = f32[128,64,128]{2,1,0:T(8,128)} fusion(f32[128,64,128]{2,1,0:T(8,128)} %bitcast.179, s32[256]{0:T(256)S(1)} %reshape.261, f32[256,64,128]{2,1,0:T(8,128)} %bitcast.175), kind=kCustom, calls=%fused_computation.2.clone.1 | custom fusion | flops 2097152 | bytes 25166848 | tf_op jit(solution)/shard_map/while/body/eval_jaxpr/scatter-add | solution.py:120
  651.9 18.0 %all_to_all.25 = bf16[64,16,128]{2,1,0:T(8,128)(2,1)S(1)} all-to-all(bf16[64,16,128]{2,1,0:T(8,128)(2,1)} %bitcast.210), channel_id=1, replica_groups=mesh['seq'=64,'rep'=4] {'seq'}, dimensions={0} | all-to-all | bytes 524288 | tf_op jit(solution)/shard_map/all_to_all | solution.py:133
  680.8 6.6 all-to-all-start.3
  691.2 155.4 %reduce-scatter.2.cloned.1.call-done = f32[16,2048]{1,0:T(8,128)} async-done(((f32[1024,2048]{1,0:T(8,128)}), f32[16,2048]{1,0:T(8,128)}) %reduce-scatter.2.cloned.1.call-update) | async-done | bytes 131088 | tf_op jit(solution)/shard_map/reduce_scatter | solution.py:138
  (120 shorter events, 124.3 us)
Async XLA Ops:
  7.2 18.7 %copy-start = (bf16[1,128,2048]{2,1,0:T(8,128)(2,1)S(1)}, bf16[1,128,2048]{2,1,0:T(8,128)(2,1)}, u32[]{:S(2)}) copy-start(bf16[1,128,2048]{2,1,0:T(8,128)(2,1)} %param.12) | copy-start | bytes 1572868
  13.6 112.6 %all-to-all-start = ((bf16[64,272,128]{2,1,0:T(8,128)(2,1)}), bf16[64,272,128]{2,1,0:T(8,128)(2,1)}, u32[]{:S(2)}, u32[]{:S(2)}) async-start(bf16[64,272,128]{2,1,0:T(8,128)(2,1)} %pad_maximum_fusion), calls=%async_computation | async-start | bytes 8912896 | tf_op jit(solution)/shard_map/all_to_all | solution.py:15
  25.8 107.5 %copy-start.7 = (s32[128,8]{0,1:T(8,128)S(1)}, s32[128,8]{0,1:T(8,128)}, u32[]{:S(2)}) copy-start(s32[128,8]{0,1:T(8,128)} %param.13) | copy-start | bytes 12292
  126.2 18.4 %all-to-all-start.1 = ((bf16[64,16,128]{2,1,0:T(8,128)(2,1)}), bf16[64,16,128]{2,1,0:T(8,128)(2,1)S(1)}, u32[]{:S(2)}, u32[]{:S(2)}) async-start(bf16[64,16,128]{2,1,0:T(8,128)(2,1)} %bitcast.37), calls=%async_computation.1 | async-start | bytes 524288 | tf_op jit(solution)/shard_map/all_to_all | solution.py:73
  133.1 713.5 %reduce-scatter.2.cloned.1.call-start = ((), (), s32[]{:S(2)}) async-start(), calls=%async_computation.6 | async-start | bytes 8519680 | tf_op jit(solution)/shard_map/reduce_scatter | solution.py:138
  149.6 15.1 %copy-start.4 = (bf16[4,32,8,1,128]{4,2,1,3,0:T(8,128)(2,1)}, bf16[4,32,8,1,128]{4,2,1,3,0:T(8,128)(2,1)S(1)}, u32[]{:S(2)}) copy-start(bf16[4,32,8,1,128]{4,2,1,3,0:T(8,128)(2,1)S(1)} %get-tuple-element.251) | copy-start | bytes 786436 | tf_op jit(solution)/shard_map/while
  161.0 3.7 copy-start.3
  164.7 2.2 copy-start.1
  235.9 39.2 %copy-start.5 = (bf16[4,32,8,1,128]{4,2,1,3,0:T(8,128)(2,1)S(1)}, bf16[4,32,8,1,128]{4,2,1,3,0:T(8,128)(2,1)}, u32[]{:S(2)}) copy-start(bf16[4,32,8,1,128]{4,2,1,3,0:T(8,128)(2,1)} %copy-done.4) | copy-start | bytes 786436 | tf_op jit(solution)/shard_map/while
  275.1 15.1 %copy-start.4 = (bf16[4,32,8,1,128]{4,2,1,3,0:T(8,128)(2,1)}, bf16[4,32,8,1,128]{4,2,1,3,0:T(8,128)(2,1)S(1)}, u32[]{:S(2)}) copy-start(bf16[4,32,8,1,128]{4,2,1,3,0:T(8,128)(2,1)S(1)} %get-tuple-element.251) | copy-start | bytes 786436 | tf_op jit(solution)/shard_map/while
  286.4 3.7 copy-start.3
  290.1 2.2 copy-start.1
  361.4 39.3 %copy-start.5 = (bf16[4,32,8,1,128]{4,2,1,3,0:T(8,128)(2,1)S(1)}, bf16[4,32,8,1,128]{4,2,1,3,0:T(8,128)(2,1)}, u32[]{:S(2)}) copy-start(bf16[4,32,8,1,128]{4,2,1,3,0:T(8,128)(2,1)} %copy-done.4) | copy-start | bytes 786436 | tf_op jit(solution)/shard_map/while
  400.8 15.1 %copy-start.4 = (bf16[4,32,8,1,128]{4,2,1,3,0:T(8,128)(2,1)}, bf16[4,32,8,1,128]{4,2,1,3,0:T(8,128)(2,1)S(1)}, u32[]{:S(2)}) copy-start(bf16[4,32,8,1,128]{4,2,1,3,0:T(8,128)(2,1)S(1)} %get-tuple-element.251) | copy-start | bytes 786436 | tf_op jit(solution)/shard_map/while
  412.1 3.7 copy-start.3
  415.8 2.2 copy-start.1
  487.1 39.2 %copy-start.5 = (bf16[4,32,8,1,128]{4,2,1,3,0:T(8,128)(2,1)S(1)}, bf16[4,32,8,1,128]{4,2,1,3,0:T(8,128)(2,1)}, u32[]{:S(2)}) copy-start(bf16[4,32,8,1,128]{4,2,1,3,0:T(8,128)(2,1)} %copy-done.4) | copy-start | bytes 786436 | tf_op jit(solution)/shard_map/while
  526.3 15.1 %copy-start.4 = (bf16[4,32,8,1,128]{4,2,1,3,0:T(8,128)(2,1)}, bf16[4,32,8,1,128]{4,2,1,3,0:T(8,128)(2,1)S(1)}, u32[]{:S(2)}) copy-start(bf16[4,32,8,1,128]{4,2,1,3,0:T(8,128)(2,1)S(1)} %get-tuple-element.251) | copy-start | bytes 786436 | tf_op jit(solution)/shard_map/while
  537.7 3.7 copy-start.3
  541.4 2.2 copy-start.1
  612.7 39.2 %copy-start.5 = (bf16[4,32,8,1,128]{4,2,1,3,0:T(8,128)(2,1)S(1)}, bf16[4,32,8,1,128]{4,2,1,3,0:T(8,128)(2,1)}, u32[]{:S(2)}) copy-start(bf16[4,32,8,1,128]{4,2,1,3,0:T(8,128)(2,1)} %copy-done.4) | copy-start | bytes 786436 | tf_op jit(solution)/shard_map/while
  674.6 3.5 copy-start.2
  677.4 1.1 copy-start.6
  680.8 166.8 %all-to-all-start.3 = ((bf16[64,272,128]{2,1,0:T(8,128)(2,1)}), bf16[64,272,128]{2,1,0:T(8,128)(2,1)}, u32[]{:S(2)}, u32[]{:S(2)}) async-start(bf16[64,272,128]{2,1,0:T(8,128)(2,1)} %pad_maximum_fusion.1), calls=%async_computation.3 | async-start | bytes 8912896 | tf_op jit(solution)/shard_map/all_to_all | solution.py:15
  848.3 11.3 %all-to-all-start.4 = ((bf16[4,16,2048]{2,1,0:T(8,128)(2,1)}), bf16[4,16,2048]{2,1,0:T(8,128)(2,1)S(1)}, u32[]{:S(2)}, u32[]{:S(2)}) async-start(bf16[4,16,2048]{2,1,0:T(8,128)(2,1)} %broadcast_in_dim.39), calls=%async_computation.5 | async-start | bytes 524288 | tf_op jit(solution)/shard_map/all_to_all | solution.py:21
Sparse Core Ops, SparseCore 0:
  674.7 171.9 reduce-scatter.1
where the time goes:
time: 875 us; the launch traced here: 867 us
  other arithmetic  327 us (37%)
  waiting for transfers between devices  257 us (29%)
  local copies, waits for them, and re-layouts  127 us (15%)
  matrix products  94.1 us (11%)
  starting transfers between devices  30.2 us (3%)
  blocking collectives  18 us (2%)
  between operations  14.2 us (2%)
    scatter-add x4, other arithmetic, attend_step(): key_acc.at[pattern_run]  157 us
    scatter-add x4, other arithmetic, attend_step(): value_acc.at[pattern_run]  157 us
    reduce_scatter x1, waiting for transfers between devices, local(): lax.psum_scatter(lax.dot_general(attended, grad_local, (((0,), (0,)), (()...  155 us
    all_to_all x2, waiting for transfers between devices, in_one_piece(): lax.all_to_all(both, axis, split_axis=split_dim, concat_axis=concat_dim,...  95.9 us
    transpose x4, local copies, waits for them, and re-layouts, attend_step(): jnp.einsum('chrk,crhd->ckhd', probs_low, grad_run, preferred_element_type...  35.8 us
    mul x4, local copies, waits for them, and re-layouts, attend_step(): jnp.einsum('chrk,crhd->ckhd', score_grad, query_run, preferred_element_ty...  35.8 us
    dot_general x4, matrix products, attend_step(): jnp.einsum('chrk,crhd->ckhd', probs_low, grad_run, preferred_element_type...  21.4 us
    dot_general x4, matrix products, attend_step(): jnp.einsum('chrk,crhd->ckhd', score_grad, query_run, preferred_element_ty...  21.4 us
  transfers between devices with their start and end apart: 5, of which 3 were waited for; matrix products, arithmetic and copies ran while one was open for 3% of the time, Pallas kernels for 0%

commit v1 on v0

v1 whole, which is shorter than its diff:
```python
import math

import jax
import jax.numpy as jnp
from jax import lax
from jax.experimental import pallas as pl
from jax.experimental.pallas import tpu as pltpu
from jax.sharding import Mesh, PartitionSpec as P

HD = 128
BLK = 64


def attend_kernel(pat_ref, q_ref, g_ref, kv_ref, o_ref, dq_ref, dkv_ref, acc_ref):
    X = lax.axis_index("x")
    C = lax.axis_index("c")
    scale = 1.0 / math.sqrt(HD)
    nt = (((1,), (1,)), ((), ()))
    tn = (((0,), (0,)), ((), ()))
    acc_ref[...] = jnp.zeros_like(acc_ref)

    def block(i, carry):
        row = X * 32 + (i // 2) * 4 + C * 2 + i % 2
        offs = []
        for j in range(8):
            p = pat_ref[row, j]
            s = p // 2
            off = ((s % 2) * 4 + s // 16) * 2048 + ((s // 2) % 8) * 128 + (p % 2) * 64
            offs.append(pl.multiple_of(off, 64))
        q = q_ref[pl.ds(pl.multiple_of(i * 64, 64), 64), :]
        g = g_ref[pl.ds(pl.multiple_of(i * 64, 64), 64), :]
        kg = jnp.concatenate([kv_ref[pl.ds(o, 64), :] for o in offs], axis=0)
        vg = jnp.concatenate([kv_ref[pl.ds(o + 1024, 64), :] for o in offs], axis=0)
        s = lax.dot_general(q, kg, nt, preferred_element_type=jnp.float32) * scale
        dp = lax.dot_general(g, vg, nt, preferred_element_type=jnp.float32)
        e = jnp.exp(s - jnp.max(s, axis=-1, keepdims=True))
        p = e / jnp.sum(e, axis=-1, keepdims=True)
        p_low = p.astype(jnp.bfloat16)
        o = jnp.dot(p_low, vg, preferred_element_type=jnp.float32)
        delta = jnp.sum(p * dp, axis=-1, keepdims=True)
        ds = (p * (dp - delta)).astype(jnp.bfloat16)
        dq = jnp.dot(ds, kg, preferred_element_type=jnp.float32) * scale
        dk = lax.dot_general(ds, q, tn, preferred_element_type=jnp.float32) * scale
        dv = lax.dot_general(p_low, g, tn, preferred_element_type=jnp.float32)
        o_ref[pl.ds(pl.multiple_of(i * 64, 64), 64), :] = o.astype(jnp.bfloat16)
        dq_ref[pl.ds(pl.multiple_of(i * 64, 64), 64), :] = dq.astype(jnp.bfloat16)
        for j in range(8):
            acc_ref[pl.ds(offs[j], 64), :] += dk[j * 64 : j * 64 + 64]
            acc_ref[pl.ds(offs[j] + 1024, 64), :] += dv[j * 64 : j * 64 + 64]
        return carry

    lax.fori_loop(0, 16, block, 0)
    dkv_ref[...] = acc_ref[...].astype(jnp.bfloat16)


def attend(pattern, q, g, kv):
    vmem = pl.BlockSpec(memory_space=pltpu.VMEM)
    return pl.pallas_call(
        attend_kernel,
        out_shape=(
            jax.ShapeDtypeStruct((1024, HD), jnp.bfloat16),
            jax.ShapeDtypeStruct((1024, HD), jnp.bfloat16),
            jax.ShapeDtypeStruct((16384, HD), jnp.bfloat16),
        ),
        in_specs=[pl.BlockSpec(memory_space=pltpu.SMEM), vmem, vmem, vmem],
        out_specs=(vmem, vmem, vmem),
        scratch_shapes=[pltpu.VMEM((16384, HD), jnp.float32)],
        compiler_params=pltpu.CompilerParams(vmem_limit_bytes=40 << 20),
        name="attend",
    )(pattern, q, g, kv)


BF = jnp.bfloat16
F32 = jnp.float32
DISTANCES = (1, 7, 2, 6, 3, 5, 4)


def ring(value, step, size):
    return lax.rem(value + step + size, size)


def remote(src, dst, send, recv, **where):
    copy = pltpu.make_async_remote_copy(
        src_ref=src,
        dst_ref=dst,
        send_sem=send,
        recv_sem=recv,
        device_id=where,
        device_id_type=pl.DeviceIdType.MESH,
    )
    copy.start()
    return copy


def greet(peers):
    barrier = pltpu.get_barrier_semaphore()
    for where in peers:
        pl.semaphore_signal(
            barrier, inc=1, device_id=where, device_id_type=pl.DeviceIdType.MESH
        )
    pl.semaphore_wait(barrier, len(peers))


def cols(index, width=128):
    return pl.ds(pl.multiple_of(index * width, width), width)


def dispatch_kernel(
    q_ref, k_ref, v_ref, grad_hbm, weight_hbm,
    kv_ref, qo_ref, go_ref,
    grad, weight, ag,
    in_sem, own_sem, zs, zr, xs, xr, cs, cr,
):
    X, Z, C = (lax.axis_index(n) for n in "xzc")
    load_w = pltpu.make_async_copy(weight_hbm, weight, in_sem.at[0])
    load_g = pltpu.make_async_copy(grad_hbm, grad, in_sem.at[1])
    load_w.start()
    load_g.start()
    right, left, other = ring(X, 1, 4), ring(X, -1, 4), 1 - C
    greet(
        [{"z": ring(Z, d, 8)} for d in DISTANCES] + [{"x": right}, {"x": left}, {"c": other}]
    )

    targets = (
        lambda z: kv_ref.at[C, X, 0, z],
        lambda z: kv_ref.at[C, X, 1, z],
        lambda z: qo_ref.at[z],
        lambda z: go_ref.at[z],
    )

    def spread(t, src):
        sent = [
            remote(
                src.at[:, cols(ring(Z, d, 8))], targets[t](Z), zs.at[t, d], zr.at[t, d],
                z=ring(Z, d, 8),
            )
            for d in DISTANCES
        ]
        own = pltpu.make_async_copy(src.at[:, cols(Z)], targets[t](Z), own_sem.at[t])
        own.start()
        return sent, own

    moved = [spread(0, k_ref), spread(1, v_ref), spread(2, q_ref)]
    load_w.wait()
    load_g.wait()
    ag[...] = lax.dot_general(
        grad[...], weight[...], (((1,), (1,)), ((), ())), preferred_element_type=F32
    ).astype(BF)
    moved.append(spread(3, ag))

    def arrived(t):
        sent, own = moved[t]
        own.wait()
        for copy in sent:
            copy.wait_recv()

    sends = []
    to_right, to_left, to_core = [], [], []
    for t in range(2):
        arrived(t)
        piece = kv_ref.at[C, X, t]
        to_right.append(remote(piece, piece, xs.at[t, 0], xr.at[t, 0], x=right))
        to_left.append(remote(piece, piece, xs.at[t, 1], xr.at[t, 1], x=left))
        to_core.append(remote(piece, piece, cs.at[t, 0], cr.at[t, 0], c=other))
    relay_right, relay_left = [], []
    for t in range(2):
        to_right[t].wait_recv()
        half = kv_ref.at[C, left, t, pl.ds(0, 4)]
        relay_right.append(remote(half, half, xs.at[t, 2], xr.at[t, 2], x=right))
        piece = kv_ref.at[C, left, t]
        to_core.append(remote(piece, piece, cs.at[t, 1], cr.at[t, 1], c=other))
        to_left[t].wait_recv()
        half = kv_ref.at[C, right, t, pl.ds(4, 4)]
        relay_left.append(remote(half, half, xs.at[t, 3], xr.at[t, 3], x=left))
        piece = kv_ref.at[C, right, t]
        to_core.append(remote(piece, piece, cs.at[t, 2], cr.at[t, 2], c=other))
    for t in range(2):
        relay_right[t].wait_recv()
        relay_left[t].wait_recv()
        piece = kv_ref.at[C, ring(X, 2, 4), t]
        to_core.append(remote(piece, piece, cs.at[t, 3], cr.at[t, 3], c=other))
    arrived(2)
    arrived(3)
    for copy in to_core:
        copy.wait_recv()
    for sent, own in moved:
        sends += sent
    for copy in sends + to_right + to_left + relay_right + relay_left + to_core:
        copy.wait_send()


def dispatch(q, k, v, grad, weight):
    vmem = pl.BlockSpec(memory_space=pltpu.VMEM)
    anywhere = pl.BlockSpec(memory_space=pl.ANY)
    dma = pltpu.SemaphoreType.DMA
    return pl.pallas_call(
        dispatch_kernel,
        out_shape=(
            jax.ShapeDtypeStruct((2, 4, 2, 8, 128, HD), BF),
            jax.ShapeDtypeStruct((8, 128, HD), BF),
            jax.ShapeDtypeStruct((8, 128, HD), BF),
        ),
        in_specs=[vmem, vmem, vmem, anywhere, anywhere],
        out_specs=(vmem, vmem, vmem),
        scratch_shapes=[
            pltpu.VMEM((128, 2048), BF),
            pltpu.VMEM((1024, 2048), BF),
            pltpu.VMEM((128, 1024), BF),
            dma((2,)),
            dma((4,)),
            dma((4, 8)),
            dma((4, 8)),
            dma((2, 4)),
            dma((2, 4)),
            dma((2, 4)),
            dma((2, 4)),
        ],
        compiler_params=pltpu.CompilerParams(
            collective_id=0, has_side_effects=True, vmem_limit_bytes=40 << 20
        ),
        name="dispatch",
    )(q, k, v, grad, weight)


def add_slabs(dst, first, *more):
    @pl.loop(0, dst.shape[0])
    def _(i):
        total = first[i].astype(F32)
        for ref in more:
            total += ref[i].astype(F32)
        dst[i] = total.astype(dst.dtype)


def combine_kernel(
    o_ref, dq_ref, dkv_ref, grad, weight_hbm,
    mixed_ref, dqo_ref, dko_ref, dvo_ref, wout_ref,
    weight, att, r, a, xin, xrel, fin, wg, wr, yrel, yin, b, xb, c1, zb, wf,
    in_sem, own_sem, zs, zr, ks, kr, xs, xr, ws, wrs, ys, yr, bs, br, vs, vr, us, ur,
):
    X, Z, C, Y = (lax.axis_index(n) for n in ("x", "z", "c", "rep"))
    load_w = pltpu.make_async_copy(weight_hbm, weight, in_sem.at[0])
    load_w.start()
    right, left, across, other = ring(X, 1, 4), ring(X, -1, 4), ring(X, 2, 4), 1 - C
    up, down, far = ring(Y, 1, 4), ring(Y, -1, 4), ring(Y, 2, 4)
    greet(
        [{"z": ring(Z, d, 8)} for d in DISTANCES]
        + [{"x": right}, {"x": left}, {"x": across}, {"c": other}]
        + [{"rep": up}, {"rep": down}, {"rep": far}]
    )

    def give(t, src, dst):
        sent = [
            remote(src.at[ring(Z, d, 8)], dst.at[:, cols(Z)], zs.at[t, d], zr.at[t, d],
                   z=ring(Z, d, 8))
            for d in DISTANCES
        ]
        own = pltpu.make_async_copy(src.at[Z], dst.at[:, cols(Z)], own_sem.at[t])
        own.start()
        return sent, own

    def arrived(moved):
        moved[1].wait()
        for copy in moved[0]:
            copy.wait_recv()

    sends = []
    att_moved = give(0, o_ref, att)
    chunk_order = (across, right, left, X)
    halves = [
        remote(dkv_ref.at[other, x], r.at[x], ks.at[n], kr.at[n], c=other)
        for n, x in enumerate(chunk_order)
    ]
    sends += halves
    dq_moved = give(1, dq_ref, dqo_ref)

    arrived(att_moved)

    @pl.loop(0, 8)
    def _(h):
        rows = lax.dot_general(
            att[:, cols(h)], grad[...], (((0,), (0,)), ((), ())), preferred_element_type=F32
        ).astype(BF)
        for n in range(8):
            for y in range(4):
                wg[n % 2, y, h * 4 + n // 2] = rows[n * 16 : n * 16 + 16, y * 512 : y * 512 + 512]

    y_order = (far, up, down, Y)
    w_halves = [
        remote(wg.at[other, y], wr.at[y], ws.at[n], wrs.at[n], c=other)
        for n, y in enumerate(y_order)
    ]
    sends += w_halves

    def add_piece(dst, *more):
        for t in range(2):
            add_slabs(dst.at[t], *[ref.at[t] for ref in more])

    halves[0].wait_recv()
    add_piece(a.at[across], dkv_ref.at[C, across], r.at[across])
    relay_a = remote(a.at[across, 0], xrel.at[0], xs.at[0], xr.at[0], x=right)
    relay_b = remote(a.at[across, 1], xrel.at[1], xs.at[1], xr.at[1], x=left)
    halves[1].wait_recv()
    add_piece(a.at[right], dkv_ref.at[C, right], r.at[right])
    near_a = remote(a.at[right, 1], xin.at[0, 1], xs.at[2], xr.at[2], x=right)
    halves[2].wait_recv()
    add_piece(a.at[left], dkv_ref.at[C, left], r.at[left])
    near_b = remote(a.at[left, 0], xin.at[1, 0], xs.at[3], xr.at[3], x=left)

    w_halves[0].wait_recv()
    add_slabs(wr.at[far], wg.at[C, far], wr.at[far])
    yrelay_a = remote(
        wr.at[far, pl.ds(0, 16)], yrel.at[0], ys.at[0], yr.at[0], rep=up
    )
    yrelay_b = remote(
        wr.at[far, pl.ds(16, 16)], yrel.at[1], ys.at[1], yr.at[1], rep=down
    )
    w_halves[1].wait_recv()
    add_slabs(wr.at[up], wg.at[C, up], wr.at[up])
    ynear_a = remote(
        wr.at[up, pl.ds(16, 16)], yin.at[0, pl.ds(16, 16)], ys.at[2], yr.at[2], rep=up
    )
    w_halves[2].wait_recv()
    add_slabs(wr.at[down], wg.at[C, down], wr.at[down])
    ynear_b = remote(
        wr.at[down, pl.ds(0, 16)], yin.at[1, pl.ds(0, 16)], ys.at[3], yr.at[3], rep=down
    )

    relay_a.wait_recv()
    add_slabs(xrel.at[0], a.at[right, 0], xrel.at[0])
    last_a = remote(xrel.at[0], xin.at[0, 0], xs.at[4], xr.at[4], x=right)
    relay_b.wait_recv()
    add_slabs(xrel.at[1], a.at[left, 1], xrel.at[1])
    last_b = remote(xrel.at[1], xin.at[1, 1], xs.at[5], xr.at[5], x=left)

    halves[3].wait_recv()
    add_piece(a.at[X], dkv_ref.at[C, X], r.at[X])

    yrelay_a.wait_recv()
    add_slabs(yrel.at[0], wr.at[up, pl.ds(0, 16)], yrel.at[0])
    ylast_a = remote(yrel.at[0], yin.at[0, pl.ds(0, 16)], ys.at[4], yr.at[4], rep=up)
    yrelay_b.wait_recv()
    add_slabs(yrel.at[1], wr.at[down, pl.ds(16, 16)], yrel.at[1])
    ylast_b = remote(yrel.at[1], yin.at[1, pl.ds(16, 16)], ys.at[5], yr.at[5], rep=down)
    w_halves[3].wait_recv()
    add_slabs(wr.at[Y], wg.at[C, Y], wr.at[Y])

    load_w.wait()
    mixed_ref[...] = jnp.dot(att[...], weight[...], preferred_element_type=F32).astype(BF)

    near_b.wait_recv()
    last_a.wait_recv()
    add_slabs(fin.at[0], a.at[X, 0], xin.at[0, 0], xin.at[1, 0])
    dk_moved = give(2, fin.at[0], dko_ref)
    near_a.wait_recv()
    last_b.wait_recv()
    add_slabs(fin.at[1], a.at[X, 1], xin.at[0, 1], xin.at[1, 1])
    dv_moved = give(3, fin.at[1], dvo_ref)

    for copy in (ynear_a, ynear_b, ylast_a, ylast_b):
        copy.wait_recv()
    add_slabs(b, wr.at[Y], yin.at[0], yin.at[1])

    def slabs(x):
        return b.at[pl.ds(pl.multiple_of(x * 8, 8), 8)]

    b_moved = [
        remote(slabs(ring(X, d, 4)), xb.at[d], bs.at[d], br.at[d], x=ring(X, d, 4))
        for d in (1, 3, 2)
    ]
    for copy in b_moved:
        copy.wait_recv()
    add_slabs(c1, slabs(X), xb.at[1], xb.at[2], xb.at[3])
    c_moved = [
        remote(c1.at[ring(Z, d, 8)], zb.at[d], vs.at[d], vr.at[d], z=ring(Z, d, 8))
        for d in DISTANCES
    ]
    for copy in c_moved:
        copy.wait_recv()
    total = c1[Z].astype(F32)
    for d in DISTANCES:
        total += zb[d].astype(F32)
    total = total * (1.0 / math.sqrt(32768))
    wf[...] = total
    wout_ref[:, cols(Y, 512)] = total
    u_moved = [
        remote(wf, wout_ref.at[:, cols(Y, 512)], us.at[d], ur.at[d], rep=ring(Y, d, 4))
        for d in (1, 3, 2)
    ]
    arrived(dq_moved)
    arrived(dk_moved)
    arrived(dv_moved)
    for copy in u_moved:
        copy.wait_recv()
    for moved in (att_moved, dq_moved, dk_moved, dv_moved):
        sends += moved[0]
    sends += [relay_a, relay_b, near_a, near_b, last_a, last_b]
    sends += [yrelay_a, yrelay_b, ynear_a, ynear_b, ylast_a, ylast_b]
    for copy in sends + b_moved + c_moved + u_moved:
        copy.wait_send()


def combine(o, dq, dkv, grad, weight):
    vmem = pl.BlockSpec(memory_space=pltpu.VMEM)
    anywhere = pl.BlockSpec(memory_space=pl.ANY)
    dma = pltpu.SemaphoreType.DMA
    return pl.pallas_call(
        combine_kernel,
        out_shape=(
            jax.ShapeDtypeStruct((128, 2048), BF),
            jax.ShapeDtypeStruct((128, 1024), BF),
            jax.ShapeDtypeStruct((128, 1024), BF),
            jax.ShapeDtypeStruct((128, 1024), BF),
            jax.ShapeDtypeStruct((16, 2048), F32),
        ),
        in_specs=[vmem, vmem, vmem, vmem, anywhere],
        out_specs=(vmem,) * 5,
        scratch_shapes=[
            pltpu.VMEM((1024, 2048), BF),
            pltpu.VMEM((128, 1024), BF),
            pltpu.VMEM((4, 2, 8, 128, HD), BF),
            pltpu.VMEM((4, 2, 8, 128, HD), BF),
            pltpu.VMEM((2, 2, 8, 128, HD), BF),
            pltpu.VMEM((2, 8, 128, HD), BF),
            pltpu.VMEM((2, 8, 128, HD), BF),
            pltpu.VMEM((2, 4, 32, 16, 512), BF),
            pltpu.VMEM((4, 32, 16, 512), BF),
            pltpu.VMEM((2, 16, 16, 512), BF),
            pltpu.VMEM((2, 32, 16, 512), BF),
            pltpu.VMEM((32, 16, 512), BF),
            pltpu.VMEM((4, 8, 16, 512), BF),
            pltpu.VMEM((8, 16, 512), BF),
            pltpu.VMEM((8, 16, 512), BF),
            pltpu.VMEM((16, 512), F32),
            dma((1,)),
            dma((4,)),
            dma((4, 8)),
            dma((4, 8)),
            dma((4,)),
            dma((4,)),
            dma((6,)),
            dma((6,)),
            dma((4,)),
            dma((4,)),
            dma((6,)),
            dma((6,)),
            dma((4,)),
            dma((4,)),
            dma((8,)),
            dma((8,)),
            dma((4,)),
            dma((4,)),
        ],
        compiler_params=pltpu.CompilerParams(
            collective_id=1, has_side_effects=True, vmem_limit_bytes=56 << 20
        ),
        name="combine",
    )(o, dq, dkv, grad, weight)


def local(query_in, key_in, value_in, out_weight, grad_out, pattern):
    kv, q, g = dispatch(query_in[0], key_in[0], value_in[0], grad_out[0], out_weight)
    o, dq, dkv = attend(
        pattern, q.reshape(1024, HD), g.reshape(1024, HD), kv.reshape(16384, HD)
    )
    mixed_out, query_grad, key_grad, value_grad, weight_grad = combine(
        o.reshape(8, 128, HD), dq.reshape(8, 128, HD), dkv.reshape(2, 4, 2, 8, 128, HD),
        grad_out[0], out_weight,
    )
    return (mixed_out[None], query_grad[None], key_grad[None], value_grad[None], weight_grad)


def solution(mesh):
    devices = mesh.devices.reshape(4, 8, 2, 4)
    inner = Mesh(devices, ("x", "z", "c", "rep"))
    seq = ("x", "z", "c")
    rows = P("rep", seq, None)
    return jax.shard_map(
        local,
        mesh=inner,
        in_specs=(rows, rows, rows, P(), rows, P()),
        out_specs=(rows, rows, rows, rows, P(seq, None)),
        check_vma=False,
    )
```

time: 875 us -> 137 us (0.16)
  other arithmetic: 327 us -> 0 us
  waiting for transfers between devices: 257 us -> 0 us
  Pallas kernels: 0 us -> 117 us
  local copies, waits for them, and re-layouts: 127 us -> 18.7 us
  matrix products: 94.1 us -> 0 us
  starting transfers between devices: 30.2 us -> 0 us
  blocking collectives: 18 us -> 0 us
  between operations: 14.2 us -> 0.68 us
    scatter-add x8 -> x0, other arithmetic: 314 us -> none  [the longest x4 157 us: attend_step(): key_acc.at[pattern_run]]
    reduce_scatter x1 -> x0, waiting for transfers between devices: 155 us -> none  [local(): lax.psum_scatter(lax.dot_general(attended, grad_local, (((0,), (0,)), (()...]
    pallas_call x0 -> x3, Pallas kernels: none -> 117 us  [the longest x1 63.9 us: combine(): pl.pallas_call(combine_kernel, out_shape=(jax.ShapeDtypeStruct((128, 2048...]
    all_to_all x4 -> x0, waiting for transfers between devices: 101 us -> none  [the longest x2 95.9 us: in_one_piece(): lax.all_to_all(both, axis, split_axis=split_dim, concat_axis=concat_dim,...]
    dot_general x23 -> x0, matrix products: 79.7 us -> none  [the longest x4 21.4 us: attend_step(): jnp.einsum('chrk,crhd->ckhd', probs_low, grad_run, preferred_element_type...]
    transpose x10 -> x0, local copies, waits for them, and re-layouts: 36.6 us -> none  [the longest x4 35.8 us: attend_step(): jnp.einsum('chrk,crhd->ckhd', probs_low, grad_run, preferred_element_type...]
    mul x4 -> x0, local copies, waits for them, and re-layouts: 35.8 us -> none  [attend_step(): jnp.einsum('chrk,crhd->ckhd', score_grad, query_run, preferred_element_ty...]
    gather x8 -> x0, local copies, waits for them, and re-layouts: 30.7 us -> none  [the longest x4 18.4 us: attend_step(): key_blocks[pattern_run]]
  transfers between devices with their start and end apart: 5 -> 0, of which waited for: 3 -> 0; matrix products, arithmetic and copies ran while one was open for 3% -> 0% of each run, Pallas kernels for 0% -> 0%
where the time goes in v1:
time: 137 us; the launch traced here: 136 us
  Pallas kernels  117 us (85%)
  local copies, waits for them, and re-layouts  18.7 us (14%)
    pallas_call x1, Pallas kernels, combine(): pl.pallas_call(combine_kernel, out_shape=(jax.ShapeDtypeStruct((128, 2048...  63.9 us
    pallas_call x1, Pallas kernels, dispatch(): pl.pallas_call(dispatch_kernel, out_shape=(jax.ShapeDtypeStruct((2, 4, 2,...  37 us
    unnamed x22, local copies, waits for them, and re-layouts  18.7 us
    pallas_call x1, Pallas kernels, attend(): pl.pallas_call(attend_kernel, out_shape=(jax.ShapeDtypeStruct((1024, HD),...  15.8 us

profile of v1, /device:TPU:2, one launch (start us, length us, event | category | flops | bytes accessed | tf_op | source)
XLA Modules:
  0.0 136.1 jit_solution(17840002027050476685)
XLA Ops:
  0.6 0.8 copy.11.pat_ref
  1.4 0.0 copy-start
  1.4 2.2 %copy-done = bf16[1024,2048]{1,0:T(8,128)(2,1)S(1)} copy-done((bf16[1024,2048]{1,0:T(8,128)(2,1)S(1)}, bf16[1024,2048]{1,0:T(8,128)(2,1)}, u32[]{:S(2)}) %copy-start) | copy-done | bytes 4194328
  3.6 0.0 copy-start.2
  3.6 1.0 copy-done.2
  4.6 0.0 copy-start.5
  4.7 0.9 copy-done.5
  5.6 0.0 copy-start.6
  5.6 0.9 copy-done.6
  6.6 0.0 copy-start.7
  6.6 0.9 copy-done.7
  7.5 37.0 %dispatch.1 = (bf16[2,4,2,8,128,128]{5,4,3,2,1,0:T(8,128)(2,1)S(1)}, bf16[8,128,128]{2,1,0:T(8,128)(2,1)S(1)}, bf16[8,128,128]{2,1,0:T(8,128)(2,1)S(1)}) custom-call(bf16[128,1024]{1,0:T(8,128)(2,1)S(1)} %bitcast.22, bf16[128,1024]{1,0:T(8,128)(2,1)S(1)} %bitcast.23, bf16[128,1024]{1,0:T(8,128)(2,1)S(1)} %bitcast.24, bf16[128,2048]{1,0:T(8,128)(2,1)S(1)} %bitcast.17, ...), custom_call_target="tpu_custom_call" | custom-call | tf_op jit(solution)/shard_map/dispatch/pallas_call | solution.py:196
  44.5 15.8 %attend.1 = (bf16[1024,128]{1,0:T(8,128)(2,1)S(1)}, bf16[1024,128]{1,0:T(8,128)(2,1)S(1)}, bf16[16384,128]{1,0:T(8,128)(2,1)S(1)}) custom-call(s32[128,8]{1,0:T(8,128)S(1)} %copy.11.pat_ref, bf16[1024,128]{1,0:T(8,128)(2,1)S(1)} %bitcast.20, bf16[1024,128]{1,0:T(8,128)(2,1)S(1)} %bitcast.21, bf16[16384,128]{1,0:T(8,128)(2,1)S(1)} %bitcast.14), custom_call_target="tpu_custom_call" | custom-call | tf_op jit(solution)/shard_map/attend/pallas_call | solution.py:58
  60.4 0.0 copy-start.1
  60.4 1.9 %copy-done.1 = bf16[16384,128]{1,0:T(8,128)(2,1)} copy-done((bf16[16384,128]{1,0:T(8,128)(2,1)}, bf16[16384,128]{1,0:T(8,128)(2,1)S(1)}, u32[]{:S(2)}) %copy-start.1) | copy-done | bytes 4194328
  62.3 0.0 copy-start.3
  62.3 0.7 copy-done.3
  63.0 0.0 copy-start.4
  63.0 0.7 copy-done.4
  63.7 63.9 %combine.1 = (bf16[128,2048]{1,0:T(8,128)(2,1)}, bf16[128,1024]{1,0:T(8,128)(2,1)}, bf16[128,1024]{1,0:T(8,128)(2,1)}, bf16[128,1024]{1,0:T(8,128)(2,1)}, f32[16,2048]{1,0:T(8,128)}) custom-call(bf16[8,128,128]{2,1,0:T(8,128)(2,1)} %bitcast.18, bf16[8,128,128]{2,1,0:T(8,128)(2,1)} %bitcast.19, bf16[2,4,2,8,128,128]{5,4,3,2,1,0:T(8,128)(2,1)} %bitcast.15, ...), custom_call_target="tpu_custom_call" | custom-call | tf_op jit(solution)/shard_map/combine/pallas_call | solution.py:406
  127.7 1.9 %copy.17 = bf16[1,128,2048]{2,1,0:T(8,128)(2,1)} copy(bf16[1,128,2048]{2,1,0:T(8,128)(2,1)} %bitcast.25) | data formatting | bytes 1048576
  129.6 1.7 %copy.18 = bf16[1,128,1024]{2,1,0:T(8,128)(2,1)} copy(bf16[1,128,1024]{2,1,0:T(8,128)(2,1)} %bitcast.28) | data formatting | bytes 524288
  131.2 1.7 %copy.19 = bf16[1,128,1024]{2,1,0:T(8,128)(2,1)} copy(bf16[1,128,1024]{2,1,0:T(8,128)(2,1)} %bitcast.27) | data formatting | bytes 524288
  132.9 1.7 %copy.20 = bf16[1,128,1024]{2,1,0:T(8,128)(2,1)} copy(bf16[1,128,1024]{2,1,0:T(8,128)(2,1)} %bitcast.26) | data formatting | bytes 524288
  134.6 1.6 %copy.21 = f32[16,2048]{1,0:T(8,128)} copy(f32[16,2048]{1,0:T(8,128)} %get-tuple-element.36) | data formatting | bytes 262144
Async XLA Ops:
  1.4 2.2 %copy-start = (bf16[1024,2048]{1,0:T(8,128)(2,1)S(1)}, bf16[1024,2048]{1,0:T(8,128)(2,1)}, u32[]{:S(2)}) copy-start(bf16[1024,2048]{1,0:T(8,128)(2,1)} %weight_hbm.3) | copy-start | bytes 12582916
  3.6 1.0 copy-start.2
  4.6 0.9 copy-start.5
  5.6 0.9 copy-start.6
  6.6 0.9 copy-start.7
  60.4 1.9 %copy-start.1 = (bf16[16384,128]{1,0:T(8,128)(2,1)}, bf16[16384,128]{1,0:T(8,128)(2,1)S(1)}, u32[]{:S(2)}) copy-start(bf16[16384,128]{1,0:T(8,128)(2,1)S(1)} %get-tuple-element.21) | copy-start | bytes 12582916
  62.3 0.7 copy-start.3
  63.0 0.7 copy-start.4

commit v2 on v0

v2 whole, which is shorter than its diff:
```python
import math

import jax
import jax.numpy as jnp
from jax import lax
from jax.experimental import pallas as pl
from jax.experimental.pallas import tpu as pltpu
from jax.sharding import Mesh, PartitionSpec as P

HD = 128
BLK = 64
BF = jnp.bfloat16
F32 = jnp.float32
SCALE = 1.0 / math.sqrt(HD)
DISTANCES = (1, 7, 2, 6, 3, 5, 4)
NT = (((1,), (1,)), ((), ()))
TN = (((0,), (0,)), ((), ()))


def ring(value, step, size):
    return lax.rem(value + step + size, size)


def link(src, dst, send, recv, **where):
    return pltpu.make_async_remote_copy(
        src_ref=src,
        dst_ref=dst,
        send_sem=send,
        recv_sem=recv,
        device_id=where,
        device_id_type=pl.DeviceIdType.MESH,
    )


def remote(src, dst, send, recv, **where):
    copy = link(src, dst, send, recv, **where)
    copy.start()
    return copy


def greet(peers):
    barrier = pltpu.get_barrier_semaphore()
    for where in peers:
        pl.semaphore_signal(
            barrier, inc=1, device_id=where, device_id_type=pl.DeviceIdType.MESH
        )
    pl.semaphore_wait(barrier, len(peers))


def span(index, width):
    return pl.ds(pl.multiple_of(index * width, width), width)


def cols(index, width=128):
    return span(index, width)


def add_slabs(dst, first, *more):
    @pl.loop(0, dst.shape[0])
    def _(i):
        total = first[i].astype(F32)
        for ref in more:
            total += ref[i].astype(F32)
        dst[i] = total.astype(dst.dtype)


def layer_kernel(
    tbl, q_hbm, k_hbm, v_hbm, grad_hbm, weight_hbm,
    mixed_hbm, dqo_ref, dko_ref, dvo_ref, wout_ref,
    q_in, k_in, v_in, grad, weight, ag, kv, qs, gs, probs, o, dq, att, segk, segv,
    given, r, a, xin, xrel, fin, wg, wr, yrel, yin, b, xb, c1, zb, wf, mixed,
    in_sem, own_sem, zs, zr, fs, fr, ks, kr, xs, xr, ws, wrs, ys, yr, bs, br, vs, vr, us, ur,
):
    X, Z, C, Y = (lax.axis_index(n) for n in ("x", "z", "c", "rep"))
    loads = [
        pltpu.make_async_copy(src, dst, in_sem.at[n])
        for n, (src, dst) in enumerate(
            ((k_hbm, k_in), (v_hbm, v_in), (q_hbm, q_in), (grad_hbm, grad), (weight_hbm, weight))
        )
    ]
    for copy in loads:
        copy.start()
    right, left, across, other = ring(X, 1, 4), ring(X, -1, 4), ring(X, 2, 4), 1 - C
    up, down, far = ring(Y, 1, 4), ring(Y, -1, 4), ring(Y, 2, 4)
    greet(
        [{"z": ring(Z, d, 8)} for d in DISTANCES]
        + [{"x": right}, {"x": left}, {"x": across}, {"c": other}]
        + [{"rep": up}, {"rep": down}, {"rep": far}]
    )

    def piece(c, x, t, first=0, count=8):
        return kv.at[pl.ds((((c * 4 + x) * 2 + t) * 8 + first) * 2, count * 2)]

    targets = (
        lambda: piece(C, X, 0, Z, 1),
        lambda: piece(C, X, 1, Z, 1),
        lambda: qs.at[pl.ds(Z * 2, 2)],
        lambda: gs.at[pl.ds(Z * 2, 2)],
    )

    def spread(t, src):
        sent = [
            remote(
                src.at[:, :, cols(ring(Z, d, 8))], targets[t](), zs.at[t, d], zr.at[t, d],
                z=ring(Z, d, 8),
            )
            for d in DISTANCES
        ]
        own = pltpu.make_async_copy(src.at[:, :, cols(Z)], targets[t](), own_sem.at[t])
        own.start()
        return sent, own

    def arrived(moved):
        moved[1].wait()
        for copy in moved[0]:
            copy.wait_recv()

    loads[0].wait()
    k_moved = spread(0, k_in)
    loads[1].wait()
    v_moved = spread(1, v_in)
    loads[2].wait()
    q_moved = spread(2, q_in)
    segk[128] = jnp.zeros((BLK, HD), F32)
    segv[128] = jnp.zeros((BLK, HD), F32)
    loads[3].wait()
    loads[4].wait()
    rows = lax.dot_general(grad[...], weight[...], NT, preferred_element_type=F32).astype(BF)
    ag[0] = rows[:64]
    ag[1] = rows[64:]
    g_moved = spread(3, ag)

    to_right, to_left, to_core = [], [], []
    for t, moved in enumerate((k_moved, v_moved)):
        arrived(moved)
        here = piece(C, X, t)
        to_right.append(remote(here, here, fs.at[t, 0], fr.at[t, 0], x=right))
        to_left.append(remote(here, here, fs.at[t, 1], fr.at[t, 1], x=left))
        to_core.append(remote(here, here, fs.at[t, 2], fr.at[t, 2], c=other))
    relays = []
    for t in range(2):
        to_right[t].wait_recv()
        half = piece(C, left, t, 0, 4)
        relays.append(remote(half, half, fs.at[t, 3], fr.at[t, 3], x=right))
        here = piece(C, left, t)
        to_core.append(remote(here, here, fs.at[t, 4], fr.at[t, 4], c=other))
        to_left[t].wait_recv()
        half = piece(C, right, t, 4, 4)
        relays.append(remote(half, half, fs.at[t, 5], fr.at[t, 5], x=left))
        here = piece(C, right, t)
        to_core.append(remote(here, here, fs.at[t, 6], fr.at[t, 6], c=other))
    for t in range(2):
        relays[2 * t].wait_recv()
        relays[2 * t + 1].wait_recv()
        here = piece(C, across, t)
        to_core.append(remote(here, here, fs.at[t, 7], fr.at[t, 7], c=other))
    arrived(q_moved)
    for copy in to_core:
        copy.wait_recv()

    def gathered(i, extra):
        return jnp.concatenate(
            [
                kv[tbl[0, i * 8 + j] + extra]
                for j in range(8)
            ],
            axis=0,
        )

    def out_copy(t, n, src, dst):
        z = lax.rem(Z + n + 1, 8)
        return link(
            src.at[span(z, 128)], dst.at[:, cols(Z)], zs.at[t, n + 1], zr.at[t, n + 1], z=z
        )

    @pl.loop(0, 8)
    def _(n):
        z = lax.rem(Z + n + 1, 8)
        for half in range(2):
            i = z * 2 + half
            rows = span(i, 64)
            s = lax.dot_general(qs[i], gathered(i, 0), NT, preferred_element_type=F32) * SCALE
            e = jnp.exp(s - jnp.max(s, axis=-1, keepdims=True))
            p = e / jnp.sum(e, axis=-1, keepdims=True)
            probs[rows, :] = p
            o[rows, :] = jnp.dot(
                p.astype(BF), gathered(i, 16), preferred_element_type=F32
            ).astype(BF)

        @pl.when(n < 7)
        def _():
            out_copy(4, n, o, att).start()

    att_own = pltpu.make_async_copy(o.at[span(Z, 128)], att.at[:, cols(Z)], own_sem.at[4])
    att_own.start()
    att_moved = [out_copy(4, n, o, att) for n in range(7)], att_own
    arrived(g_moved)

    def backward(first, last):
        @pl.loop(first, last)
        def _(n):
            z = lax.rem(Z + n + 1, 8)
            for half in range(2):
                i = z * 2 + half
                rows = span(i, 64)
                q, g, p = qs[i], gs[i], probs[rows, :]
                kg = gathered(i, 0)
                dp = lax.dot_general(g, gathered(i, 16), NT, preferred_element_type=F32)
                delta = jnp.sum(p * dp, axis=-1, keepdims=True)
                ds = (p * (dp - delta)).astype(BF)
                dq[rows, :] = (
                    jnp.dot(ds, kg, preferred_element_type=F32) * SCALE
                ).astype(BF)
                dk = lax.dot_general(ds, q, TN, preferred_element_type=F32)
                dv = lax.dot_general(p.astype(BF), g, TN, preferred_element_type=F32)
                m = n * 2 + half
                for j in range(8):
                    before = tbl[1, m * 8 + j]
                    segk[m * 8 + j] = segk[before] + dk[j * 64 : j * 64 + 64]
                    segv[m * 8 + j] = segv[before] + dv[j * 64 : j * 64 + 64]

            @pl.when(n < 7)
            def _():
                out_copy(5, n, dq, dqo_ref).start()

    backward(0, 4)
    arrived(att_moved)

    @pl.loop(0, 8)
    def _(h):
        rows = lax.dot_general(att[:, cols(h)], grad[...], TN, preferred_element_type=F32).astype(BF)
        for n in range(8):
            for y in range(4):
                wg[n % 2, y, h * 4 + n // 2] = rows[n * 16 : n * 16 + 16, y * 512 : y * 512 + 512]

    w_halves = [
        remote(wg.at[other, y], wr.at[y], ws.at[n], wrs.at[n], c=other)
        for n, y in enumerate((far, up, down, Y))
    ]
    backward(4, 6)

    low, high = pl.ds(0, 16), pl.ds(16, 16)
    w_halves[0].wait_recv()
    add_slabs(wr.at[far], wg.at[C, far], wr.at[far])
    yrelay_a = remote(wr.at[far, low], yrel.at[0], ys.at[0], yr.at[0], rep=up)
    yrelay_b = remote(wr.at[far, high], yrel.at[1], ys.at[1], yr.at[1], rep=down)
    w_halves[1].wait_recv()
    add_slabs(wr.at[up], wg.at[C, up], wr.at[up])
    ynear_a = remote(wr.at[up, high], yin.at[0, high], ys.at[2], yr.at[2], rep=up)
    w_halves[2].wait_recv()
    add_slabs(wr.at[down], wg.at[C, down], wr.at[down])
    ynear_b = remote(wr.at[down, low], yin.at[1, low], ys.at[3], yr.at[3], rep=down)
    w_halves[3].wait_recv()
    add_slabs(wr.at[Y], wg.at[C, Y], wr.at[Y])

    backward(6, 8)
    dq_own = pltpu.make_async_copy(dq.at[span(Z, 128)], dqo_ref.at[:, cols(Z)], own_sem.at[5])
    dq_own.start()
    dq_moved = [out_copy(5, n, dq, dqo_ref) for n in range(7)], dq_own

    def collect(x, core, dst, more=None):
        @pl.loop(0, 8)
        def _(z):
            for half in range(2):
                slot = tbl[2, x * 32 + z * 4 + core * 2 + half]
                rows = slice(half * 64, half * 64 + 64)
                for t, total in enumerate((segk[slot] * SCALE, segv[slot])):
                    if more is not None:
                        total += more[t, z, rows].astype(F32)
                    dst[t, z, rows] = total.astype(BF)

    halves = []
    for n, x in enumerate((across, right, left, X)):
        collect(x, other, given.at[x])
        halves.append(remote(given.at[x], r.at[x], ks.at[n], kr.at[n], c=other))

    halves[0].wait_recv()
    collect(across, C, a.at[across], r.at[across])
    relay_a = remote(a.at[across, 0], xrel.at[0], xs.at[0], xr.at[0], x=right)
    relay_b = remote(a.at[across, 1], xrel.at[1], xs.at[1], xr.at[1], x=left)
    halves[1].wait_recv()
    collect(right, C, a.at[right], r.at[right])
    near_a = remote(a.at[right, 1], xin.at[0, 1], xs.at[2], xr.at[2], x=right)
    halves[2].wait_recv()
    collect(left, C, a.at[left], r.at[left])
    near_b = remote(a.at[left, 0], xin.at[1, 0], xs.at[3], xr.at[3], x=left)

    yrelay_a.wait_recv()
    add_slabs(yrel.at[0], wr.at[up, low], yrel.at[0])
    ylast_a = remote(yrel.at[0], yin.at[0, low], ys.at[4], yr.at[4], rep=up)
    yrelay_b.wait_recv()
    add_slabs(yrel.at[1], wr.at[down, high], yrel.at[1])
    ylast_b = remote(yrel.at[1], yin.at[1, high], ys.at[5], yr.at[5], rep=down)

    halves[3].wait_recv()
    collect(X, C, a.at[X], r.at[X])
    mixed[...] = jnp.dot(att[...], weight[...], preferred_element_type=F32).astype(BF)
    mixed_out = pltpu.make_async_copy(mixed, mixed_hbm, in_sem.at[5])
    mixed_out.start()

    relay_a.wait_recv()
    add_slabs(xrel.at[0], a.at[right, 0], xrel.at[0])
    last_a = remote(xrel.at[0], xin.at[0, 0], xs.at[4], xr.at[4], x=right)
    relay_b.wait_recv()
    add_slabs(xrel.at[1], a.at[left, 1], xrel.at[1])
    last_b = remote(xrel.at[1], xin.at[1, 1], xs.at[5], xr.at[5], x=left)

    for copy in (ynear_a, ynear_b, ylast_a, ylast_b):
        copy.wait_recv()
    add_slabs(b, wr.at[Y], yin.at[0], yin.at[1])

    def slabs(x):
        return b.at[span(x, 8)]

    b_moved = [
        remote(slabs(ring(X, d, 4)), xb.at[d], bs.at[d], br.at[d], x=ring(X, d, 4))
        for d in (1, 3, 2)
    ]

    def give(t, src, dst):
        sent = [
            remote(src.at[ring(Z, d, 8)], dst.at[:, cols(Z)], zs.at[t, d], zr.at[t, d],
                   z=ring(Z, d, 8))
            for d in DISTANCES
        ]
        own = pltpu.make_async_copy(src.at[Z], dst.at[:, cols(Z)], own_sem.at[t])
        own.start()
        return sent, own

    near_b.wait_recv()
    last_a.wait_recv()
    add_slabs(fin.at[0], a.at[X, 0], xin.at[0, 0], xin.at[1, 0])
    dk_moved = give(6, fin.at[0], dko_ref)
    near_a.wait_recv()
    last_b.wait_recv()
    add_slabs(fin.at[1], a.at[X, 1], xin.at[0, 1], xin.at[1, 1])
    dv_moved = give(7, fin.at[1], dvo_ref)

    for copy in b_moved:
        copy.wait_recv()
    add_slabs(c1, slabs(X), xb.at[1], xb.at[2], xb.at[3])
    c_moved = [
        remote(c1.at[ring(Z, d, 8)], zb.at[d], vs.at[d], vr.at[d], z=ring(Z, d, 8))
        for d in DISTANCES
    ]
    for copy in c_moved:
        copy.wait_recv()
    total = c1[Z].astype(F32)
    for d in DISTANCES:
        total += zb[d].astype(F32)
    wf[...] = total * (1.0 / math.sqrt(32768))
    w_own = pltpu.make_async_copy(wf, wout_ref.at[:, cols(Y, 512)], in_sem.at[6])
    w_own.start()
    u_moved = [
        remote(wf, wout_ref.at[:, cols(Y, 512)], us.at[d], ur.at[d], rep=ring(Y, d, 4))
        for d in (1, 3, 2)
    ]
    arrived(dq_moved)
    arrived(dk_moved)
    arrived(dv_moved)
    for copy in u_moved:
        copy.wait_recv()
    w_own.wait()
    mixed_out.wait()
    sends = []
    for moved in (k_moved, v_moved, q_moved, g_moved, att_moved, dq_moved, dk_moved, dv_moved):
        sends += moved[0]
    sends += to_right + to_left + to_core + relays + w_halves + halves
    sends += [relay_a, relay_b, near_a, near_b, last_a, last_b]
    sends += [yrelay_a, yrelay_b, ynear_a, ynear_b, ylast_a, ylast_b]
    for copy in sends + b_moved + c_moved + u_moved:
        copy.wait_send()


OUTPUTS = (
    jax.ShapeDtypeStruct((128, 2048), BF),
    jax.ShapeDtypeStruct((128, 1024), BF),
    jax.ShapeDtypeStruct((128, 1024), BF),
    jax.ShapeDtypeStruct((128, 1024), BF),
    jax.ShapeDtypeStruct((16, 2048), F32),
)


def layer(tables, q, k, v, grad, weight):
    anywhere = pl.BlockSpec(memory_space=pl.ANY)
    dma = pltpu.SemaphoreType.DMA
    vm = pltpu.VMEM
    return pl.pallas_call(
        layer_kernel,
        out_shape=OUTPUTS,
        in_specs=[pl.BlockSpec(memory_space=pltpu.SMEM)] + [anywhere] * 5,
        out_specs=(anywhere,) * 5,
        scratch_shapes=[
            vm((2, BLK, 1024), BF),
            vm((2, BLK, 1024), BF),
            vm((2, BLK, 1024), BF),
            vm((128, 2048), BF),
            vm((1024, 2048), BF),
            vm((2, BLK, 1024), BF),
            vm((256, BLK, HD), BF),
            vm((16, BLK, HD), BF),
            vm((16, BLK, HD), BF),
            vm((1024, 512), F32),
            vm((1024, HD), BF),
            vm((1024, HD), BF),
            vm((128, 1024), BF),
            vm((129, BLK, HD), F32),
            vm((129, BLK, HD), F32),
            vm((4, 2, 8, 128, HD), BF),
            vm((4, 2, 8, 128, HD), BF),
            vm((4, 2, 8, 128, HD), BF),
            vm((2, 2, 8, 128, HD), BF),
            vm((2, 8, 128, HD), BF),
            vm((2, 8, 128, HD), BF),
            vm((2, 4, 32, 16, 512), BF),
            vm((4, 32, 16, 512), BF),
            vm((2, 16, 16, 512), BF),
            vm((2, 32, 16, 512), BF),
            vm((32, 16, 512), BF),
            vm((4, 8, 16, 512), BF),
            vm((8, 16, 512), BF),
            vm((8, 16, 512), BF),
            vm((16, 512), F32),
            vm((128, 2048), BF),
            dma((7,)),
            dma((8,)),
            dma((8, 8)),
            dma((8, 8)),
            dma((2, 8)),
            dma((2, 8)),
            dma((4,)),
            dma((4,)),
            dma((6,)),
            dma((6,)),
            dma((4,)),
            dma((4,)),
            dma((6,)),
            dma((6,)),
            dma((4,)),
            dma((4,)),
            dma((8,)),
            dma((8,)),
            dma((4,)),
            dma((4,)),
        ],
        compiler_params=pltpu.CompilerParams(
            collective_id=0, has_side_effects=True, vmem_limit_bytes=63 << 20
        ),
        name="layer",
    )(tables, q, k, v, grad, weight)


def finish_kernel(*refs):
    sources, results, held, sems = refs[:5], refs[5:10], refs[10:15], refs[15]
    taken = [
        pltpu.make_async_copy(src, buf, sems.at[n])
        for n, (src, buf) in enumerate(zip(sources, held))
    ]
    put = [
        pltpu.make_async_copy(buf, dst, sems.at[5 + n])
        for n, (buf, dst) in enumerate(zip(held, results))
    ]
    for copy in taken:
        copy.start()
    for copy, onward in zip(taken, put):
        copy.wait()
        onward.start()
    for copy in put:
        copy.wait()


def finish(arrays):
    anywhere = pl.BlockSpec(memory_space=pl.ANY)
    return pl.pallas_call(
        finish_kernel,
        out_shape=OUTPUTS,
        in_specs=[anywhere] * 5,
        out_specs=(anywhere,) * 5,
        scratch_shapes=[pltpu.VMEM(s.shape, s.dtype) for s in OUTPUTS]
        + [pltpu.SemaphoreType.DMA((10,))],
        compiler_params=pltpu.CompilerParams(vmem_limit_bytes=63 << 20),
        name="finish",
    )(*arrays)


def tables_of(pattern):
    X, Z, C = (lax.axis_index(n) for n in "xzc")
    by_owner = pattern.reshape(4, 8, 2, 16)
    mine = lax.dynamic_slice(by_owner, (X, 0, C, 0), (1, 8, 1, 16)).reshape(8, 16)
    plain = mine.reshape(128)
    turned = jnp.concatenate([mine, mine], axis=0)
    turned = lax.dynamic_slice(turned, (lax.rem(Z + 1, 8), 0), (8, 16)).reshape(128)
    s = plain // 2
    places = ((s % 2) * 4 + s // 16) * 32 + ((s // 2) % 8) * 2 + plain % 2
    order = jnp.arange(128, dtype=jnp.int32)
    same = turned[None, :] == turned[:, None]
    earlier = order[None, :] < order[:, None]
    before = jnp.max(jnp.where(same & earlier, order[None, :], -1), axis=1)
    last = jnp.max(jnp.where(turned[None, :] == order[:, None], order[None, :], -1), axis=1)
    return jnp.stack(
        [places, jnp.where(before < 0, 128, before), jnp.where(last < 0, 128, last)]
    )


def local(query_in, key_in, value_in, out_weight, grad_out, pattern):
    results = layer(
        tables_of(pattern),
        *(a.reshape(2, BLK, 1024) for a in (query_in, key_in, value_in)),
        grad_out[0],
        out_weight,
    )
    mixed_out, query_grad, key_grad, value_grad, weight_grad = finish(results)
    return (mixed_out[None], query_grad[None], key_grad[None], value_grad[None], weight_grad)


def solution(mesh):
    devices = mesh.devices.reshape(4, 8, 2, 4)
    inner = Mesh(devices, ("x", "z", "c", "rep"))
    seq = ("x", "z", "c")
    rows = P("rep", seq, None)
    return jax.shard_map(
        local,
        mesh=inner,
        in_specs=(rows, rows, rows, P(), rows, P()),
        out_specs=(rows, rows, rows, rows, P(seq, None)),
        check_vma=False,
    )
```

time: 875 us -> 111 us (0.13)
  other arithmetic: 327 us -> 0.82 us
  waiting for transfers between devices: 257 us -> 0 us
  local copies, waits for them, and re-layouts: 127 us -> 2.21 us
  Pallas kernels: 0 us -> 105 us
  matrix products: 94.1 us -> 0 us
  starting transfers between devices: 30.2 us -> 0 us
  blocking collectives: 18 us -> 0 us
  between operations: 14.2 us -> 0.68 us
    scatter-add x8 -> x0, other arithmetic: 314 us -> none  [the longest x4 157 us: attend_step(): key_acc.at[pattern_run]]
    reduce_scatter x1 -> x0, waiting for transfers between devices: 155 us -> none  [local(): lax.psum_scatter(lax.dot_general(attended, grad_local, (((0,), (0,)), (()...]
    pallas_call x0 -> x2, Pallas kernels: none -> 105 us  [the longest x1 103 us: layer(): pl.pallas_call(layer_kernel, out_shape=OUTPUTS, in_specs=[pl.BlockSpec(me...]
    all_to_all x4 -> x0, waiting for transfers between devices: 101 us -> none  [the longest x2 95.9 us: in_one_piece(): lax.all_to_all(both, axis, split_axis=split_dim, concat_axis=concat_dim,...]
    dot_general x23 -> x0, matrix products: 79.7 us -> none  [the longest x4 21.4 us: attend_step(): jnp.einsum('chrk,crhd->ckhd', probs_low, grad_run, preferred_element_type...]
    transpose x10 -> x0, local copies, waits for them, and re-layouts: 36.6 us -> none  [the longest x4 35.8 us: attend_step(): jnp.einsum('chrk,crhd->ckhd', probs_low, grad_run, preferred_element_type...]
    mul x4 -> x0, local copies, waits for them, and re-layouts: 35.8 us -> none  [attend_step(): jnp.einsum('chrk,crhd->ckhd', score_grad, query_run, preferred_element_ty...]
    gather x8 -> x0, local copies, waits for them, and re-layouts: 30.7 us -> none  [the longest x4 18.4 us: attend_step(): key_blocks[pattern_run]]
  transfers between devices with their start and end apart: 5 -> 0, of which waited for: 3 -> 0; matrix products, arithmetic and copies ran while one was open for 3% -> 0% of each run, Pallas kernels for 0% -> 0%
where the time goes in v2:
time: 111 us; the launch traced here: 109 us
  Pallas kernels  105 us (95%)
  local copies, waits for them, and re-layouts  2.21 us (2%)
    pallas_call x1, Pallas kernels, layer(): pl.pallas_call(layer_kernel, out_shape=OUTPUTS, in_specs=[pl.BlockSpec(me...  103 us

profile of v2, /device:TPU:2, one launch (start us, length us, event | category | flops | bytes accessed | tf_op | source)
XLA Modules:
  0.0 109.0 jit_solution(1574514429801057124)
XLA Ops:
  0.6 0.8 copy.12
  1.4 0.1 reshape.287
  1.5 0.5 broadcast.284
  2.0 0.7 fusion.8
  2.7 0.1 reshape_reshape.3
  2.8 0.1 eq.14
  2.9 0.2 select_reduce_fusion.1
  3.1 0.6 pad_add_fusion.tbl
  3.7 103.0 %layer.1 = (bf16[128,2048]{1,0:T(8,128)(2,1)}, bf16[128,1024]{1,0:T(8,128)(2,1)}, bf16[128,1024]{1,0:T(8,128)(2,1)}, bf16[128,1024]{1,0:T(8,128)(2,1)}, f32[16,2048]{1,0:T(8,128)}) custom-call(s32[3,128]{1,0:T(4,128)} %pad_add_fusion.tbl, bf16[2,64,1024]{2,1,0:T(8,128)(2,1)} %bitcast.14, bf16[2,64,1024]{2,1,0:T(8,128)(2,1)} %bitcast.15, ...), custom_call_target="tpu_custom_call" | custom-call | tf_op jit(solution)/shard_map/layer/pallas_call | solution.py:388
  106.7 2.2 %finish.1 = (bf16[128,2048]{1,0:T(8,128)(2,1)}, bf16[128,1024]{1,0:T(8,128)(2,1)}, bf16[128,1024]{1,0:T(8,128)(2,1)}, bf16[128,1024]{1,0:T(8,128)(2,1)}, f32[16,2048]{1,0:T(8,128)}) custom-call(bf16[128,2048]{1,0:T(8,128)(2,1)} %get-tuple-element.15.refs_0_, bf16[128,1024]{1,0:T(8,128)(2,1)} %get-tuple-element.16.refs_1_, ...), custom_call_target="tpu_custom_call" | custom-call | tf_op jit(solution)/shard_map/finish/pallas_call | solution.py:474
  (3 shorter events, 0.1 us)

commit v3 on v2

--- a/solution.py
+++ b/solution.py
@@ -13,6 +13,7 @@
 F32 = jnp.float32
 SCALE = 1.0 / math.sqrt(HD)
 DISTANCES = (1, 7, 2, 6, 3, 5, 4)
+ARRIVALS = (0,) + DISTANCES
 NT = (((1,), (1,)), ((), ()))
 TN = (((0,), (0,)), ((), ()))
 
@@ -68,8 +69,8 @@
     tbl, q_hbm, k_hbm, v_hbm, grad_hbm, weight_hbm,
     mixed_hbm, dqo_ref, dko_ref, dvo_ref, wout_ref,
     q_in, k_in, v_in, grad, weight, ag, kv, qs, gs, probs, o, dq, att, segk, segv,
-    given, r, a, xin, xrel, fin, wg, wr, yrel, yin, b, xb, c1, zb, wf, mixed,
-    in_sem, own_sem, zs, zr, fs, fr, ks, kr, xs, xr, ws, wrs, ys, yr, bs, br, vs, vr, us, ur,
+    given, r, a, xin, xrel, fin, wg, wr, yrel, yin, b, xb, c1, zb, wf, mixed, turned,
+    in_sem, own_sem, zs, zr, fs, fr, cs, cr, ks, kr, xs, xr, ws, wrs, ys, yr, bs, br, vs, vr, us, ur,
 ):
     X, Z, C, Y = (lax.axis_index(n) for n in ("x", "z", "c", "rep"))
     loads = [
@@ -130,30 +131,47 @@
     ag[1] = rows[64:]
     g_moved = spread(3, ag)
 
-    to_right, to_left, to_core = [], [], []
-    for t, moved in enumerate((k_moved, v_moved)):
-        arrived(moved)
-        here = piece(C, X, t)
-        to_right.append(remote(here, here, fs.at[t, 0], fr.at[t, 0], x=right))
-        to_left.append(remote(here, here, fs.at[t, 1], fr.at[t, 1], x=left))
-        to_core.append(remote(here, here, fs.at[t, 2], fr.at[t, 2], c=other))
-    relays = []
+    near, relays, to_core = {}, {}, []
+
+    def send_near(t, d):
+        if d == 0:
+            moves[t][1].wait()
+        else:
+            moves[t][0][DISTANCES.index(d)].wait_recv()
+        here = piece(C, X, t, ring(Z, -d, 8), 1)
+        near[t, d] = (
+            remote(here, here, fs.at[t, d, 0], fr.at[t, d, 0], x=right),
+            remote(here, here, fs.at[t, d, 1], fr.at[t, d, 1], x=left),
+        )
+
+    def send_relay(t, d):
+        for copy in near[t, d]:
+            copy.wait_recv()
+        source, target = (left, right) if d < 4 else (right, left)
+        here = piece(C, source, t, ring(Z, -d, 8), 1)
+        relays[t, d] = remote(here, here, fs.at[t, d, 2], fr.at[t, d, 2], x=target)
+
+    def across_core(t, n, x):
+        here = piece(C, x, t)
+        to_core.append(remote(here, here, cs.at[t, n], cr.at[t, n], c=other))
+
+    moves = (k_moved, v_moved)
+    steps = [(t, d) for t in range(2) for d in ARRIVALS]
+    for n in range(len(steps) + 4):
+        if n < len(steps):
+            send_near(*steps[n])
+            if n % 8 == 7:
+                across_core(n // 8, 0, X)
+        if n >= 4:
+            send_relay(*steps[n - 4])
+            if n % 8 == 3:
+                across_core(n // 8 - 1, 1, left)
+                across_core(n // 8 - 1, 2, right)
     for t in range(2):
-        to_right[t].wait_recv()
-        half = piece(C, left, t, 0, 4)
-        relays.append(remote(half, half, fs.at[t, 3], fr.at[t, 3], x=right))
-        here = piece(C, left, t)
-        to_core.append(remote(here, here, fs.at[t, 4], fr.at[t, 4], c=other))
-        to_left[t].wait_recv()
-        half = piece(C, right, t, 4, 4)
-        relays.append(remote(half, half, fs.at[t, 5], fr.at[t, 5], x=left))
-        here = piece(C, right, t)
-        to_core.append(remote(here, here, fs.at[t, 6], fr.at[t, 6], c=other))
-    for t in range(2):
-        relays[2 * t].wait_recv()
-        relays[2 * t + 1].wait_recv()
-        here = piece(C, across, t)
-        to_core.append(remote(here, here, fs.at[t, 7], fr.at[t, 7], c=other))
+        for d in ARRIVALS:
+            relays[t, d].wait_recv()
+            here = piece(C, across, t, ring(Z, -d, 8), 1)
+            to_core.append(remote(here, here, cs.at[t, 3 + d], cr.at[t, 3 + d], c=other))
     arrived(q_moved)
     for copy in to_core:
         copy.wait_recv()
@@ -223,99 +241,155 @@
             def _():
                 out_copy(5, n, dq, dqo_ref).start()
 
-    backward(0, 4)
-    arrived(att_moved)
-
-    @pl.loop(0, 8)
-    def _(h):
-        rows = lax.dot_general(att[:, cols(h)], grad[...], TN, preferred_element_type=F32).astype(BF)
-        for n in range(8):
-            for y in range(4):
-                wg[n % 2, y, h * 4 + n // 2] = rows[n * 16 : n * 16 + 16, y * 512 : y * 512 + 512]
-
-    w_halves = [
-        remote(wg.at[other, y], wr.at[y], ws.at[n], wrs.at[n], c=other)
-        for n, y in enumerate((far, up, down, Y))
-    ]
-    backward(4, 6)
-
-    low, high = pl.ds(0, 16), pl.ds(16, 16)
-    w_halves[0].wait_recv()
-    add_slabs(wr.at[far], wg.at[C, far], wr.at[far])
-    yrelay_a = remote(wr.at[far, low], yrel.at[0], ys.at[0], yr.at[0], rep=up)
-    yrelay_b = remote(wr.at[far, high], yrel.at[1], ys.at[1], yr.at[1], rep=down)
-    w_halves[1].wait_recv()
-    add_slabs(wr.at[up], wg.at[C, up], wr.at[up])
-    ynear_a = remote(wr.at[up, high], yin.at[0, high], ys.at[2], yr.at[2], rep=up)
-    w_halves[2].wait_recv()
-    add_slabs(wr.at[down], wg.at[C, down], wr.at[down])
-    ynear_b = remote(wr.at[down, low], yin.at[1, low], ys.at[3], yr.at[3], rep=down)
-    w_halves[3].wait_recv()
-    add_slabs(wr.at[Y], wg.at[C, Y], wr.at[Y])
-
-    backward(6, 8)
+    backward(0, 8)
     dq_own = pltpu.make_async_copy(dq.at[span(Z, 128)], dqo_ref.at[:, cols(Z)], own_sem.at[5])
     dq_own.start()
     dq_moved = [out_copy(5, n, dq, dqo_ref) for n in range(7)], dq_own
-
-    def collect(x, core, dst, more=None):
+    arrived(att_moved)
+
+    def collect(x, core, t, dst, more=None):
         @pl.loop(0, 8)
         def _(z):
             for half in range(2):
                 slot = tbl[2, x * 32 + z * 4 + core * 2 + half]
                 rows = slice(half * 64, half * 64 + 64)
-                for t, total in enumerate((segk[slot] * SCALE, segv[slot])):
-                    if more is not None:
-                        total += more[t, z, rows].astype(F32)
-                    dst[t, z, rows] = total.astype(BF)
-
-    halves = []
-    for n, x in enumerate((across, right, left, X)):
-        collect(x, other, given.at[x])
-        halves.append(remote(given.at[x], r.at[x], ks.at[n], kr.at[n], c=other))
-
-    halves[0].wait_recv()
-    collect(across, C, a.at[across], r.at[across])
-    relay_a = remote(a.at[across, 0], xrel.at[0], xs.at[0], xr.at[0], x=right)
-    relay_b = remote(a.at[across, 1], xrel.at[1], xs.at[1], xr.at[1], x=left)
-    halves[1].wait_recv()
-    collect(right, C, a.at[right], r.at[right])
-    near_a = remote(a.at[right, 1], xin.at[0, 1], xs.at[2], xr.at[2], x=right)
-    halves[2].wait_recv()
-    collect(left, C, a.at[left], r.at[left])
-    near_b = remote(a.at[left, 0], xin.at[1, 0], xs.at[3], xr.at[3], x=left)
-
-    yrelay_a.wait_recv()
-    add_slabs(yrel.at[0], wr.at[up, low], yrel.at[0])
-    ylast_a = remote(yrel.at[0], yin.at[0, low], ys.at[4], yr.at[4], rep=up)
-    yrelay_b.wait_recv()
-    add_slabs(yrel.at[1], wr.at[down, high], yrel.at[1])
-    ylast_b = remote(yrel.at[1], yin.at[1, high], ys.at[5], yr.at[5], rep=down)
-
-    halves[3].wait_recv()
-    collect(X, C, a.at[X], r.at[X])
+                total = segk[slot] * SCALE if t == 0 else segv[slot]
+                if more is not None:
+                    total += more[z, rows].astype(F32)
+                dst[z, rows] = total.astype(BF)
+
+    w_halves, halves, ymoves = {}, {}, {}
+
+    turned[...] = att[...].T
+
+    def share_weight(h, n, y):
+        @pl.loop(0, 4)
+        def _(m):
+            rows = jnp.dot(
+                turned[span(m, 256), :], grad[:, cols(y * 2 + h, 256)], preferred_element_type=F32
+            ).astype(BF)
+            for k in range(16):
+                wg[h, k % 2, y, m * 8 + k // 2] = rows[k * 16 : k * 16 + 16]
+
+        w_halves[h, n] = remote(
+            wg.at[h, other, y], wr.at[h, y], ws.at[h, n], wrs.at[h, n], c=other
+        )
+
+    def share_keys(t):
+        for n, x in enumerate((across, right, left, X)):
+            collect(x, other, t, given.at[x, t])
+            halves[t, n] = remote(given.at[x, t], r.at[x, t], ks.at[t, n], kr.at[t, n], c=other)
+
+    def take(t, n, x):
+        halves[t, n].wait_recv()
+        collect(x, C, t, a.at[x, t], r.at[x, t])
+
+    first, second = pl.ds(0, 4), pl.ds(4, 4)
+    xmoves = {}
+
+    def xsend(name, t, n, src, dst, target):
+        xmoves[name, t] = remote(src, dst, xs.at[t, n], xr.at[t, n], x=target)
+
+    def chunk_across(t):
+        take(t, 0, across)
+        xsend("relay_a", t, 0, a.at[across, t, first], xrel.at[0, t], right)
+        xsend("relay_b", t, 1, a.at[across, t, second], xrel.at[1, t], left)
+
+    def chunks_near(t):
+        take(t, 1, right)
+        xsend("near_a", t, 2, a.at[right, t, second], xin.at[0, t, second], right)
+        take(t, 2, left)
+        xsend("near_b", t, 3, a.at[left, t, first], xin.at[1, t, first], left)
+
+    def weight_chunk(h, n, y):
+        w_halves[h, n].wait_recv()
+        add_slabs(wr.at[h, y], wg.at[h, C, y], wr.at[h, y])
+
+    low, high = pl.ds(0, 16), pl.ds(16, 16)
+
+    def ysend(name, h, n, src, dst, target):
+        ymoves[name, h] = remote(src, dst, ys.at[h, n], yr.at[h, n], rep=target)
+
+    def weight_far(h):
+        weight_chunk(h, 0, far)
+        ysend("relay_a", h, 0, wr.at[h, far, low], yrel.at[h, 0], up)
+        ysend("relay_b", h, 1, wr.at[h, far, high], yrel.at[h, 1], down)
+
+    def weight_near(h):
+        weight_chunk(h, 1, up)
+        ysend("near_a", h, 2, wr.at[h, up, high], yin.at[h, 0, high], up)
+        weight_chunk(h, 2, down)
+        ysend("near_b", h, 3, wr.at[h, down, low], yin.at[h, 1, low], down)
+
+    def weight_last(h):
+        ymoves["relay_a", h].wait_recv()
+        add_slabs(yrel.at[h, 0], wr.at[h, up, low], yrel.at[h, 0])
+        ysend("last_a", h, 4, yrel.at[h, 0], yin.at[h, 0, low], up)
+        ymoves["relay_b", h].wait_recv()
+        add_slabs(yrel.at[h, 1], wr.at[h, down, high], yrel.at[h, 1])
+        ysend("last_b", h, 5, yrel.at[h, 1], yin.at[h, 1, high], down)
+
+    b_moved = {}
+
+    def slabs(h, x):
+        return b.at[h, span(x, 8)]
+
+    def weight_rows(h):
+        for name in ("near_a", "near_b", "last_a", "last_b"):
+            ymoves[name, h].wait_recv()
+        add_slabs(b.at[h], wr.at[h, Y], yin.at[h, 0], yin.at[h, 1])
+        for d in (1, 3, 2):
+            b_moved[h, d] = remote(
+                slabs(h, ring(X, d, 4)), xb.at[h, d], bs.at[h, d], br.at[h, d], x=ring(X, d, 4)
+            )
+
+    def xpass(t):
+        xmoves["relay_a", t].wait_recv()
+        add_slabs(xrel.at[0, t], a.at[right, t, first], xrel.at[0, t])
+        xsend("last_a", t, 4, xrel.at[0, t], xin.at[0, t, first], right)
+        xmoves["relay_b", t].wait_recv()
+        add_slabs(xrel.at[1, t], a.at[left, t, second], xrel.at[1, t])
+        xsend("last_b", t, 5, xrel.at[1, t], xin.at[1, t, second], left)
+
+    share_weight(0, 0, far)
+    share_keys(0)
+    weight_far(0)
+    chunk_across(0)
+    share_weight(0, 1, up)
+    share_weight(0, 2, down)
+    chunks_near(0)
+    weight_near(0)
+    share_keys(1)
+    share_weight(1, 0, far)
+    chunk_across(1)
+    weight_far(1)
+    chunks_near(1)
+    weight_last(0)
+    xpass(0)
+    share_weight(1, 1, up)
+    share_weight(1, 2, down)
+    weight_near(1)
+    share_weight(0, 3, Y)
+    share_weight(1, 3, Y)
+    weight_last(1)
+    xpass(1)
+    weight_chunk(0, 3, Y)
+    weight_rows(0)
+    weight_chunk(1, 3, Y)
+    take(0, 3, X)
+    take(1, 3, X)
     mixed[...] = jnp.dot(att[...], weight[...], preferred_element_type=F32).astype(BF)
     mixed_out = pltpu.make_async_copy(mixed, mixed_hbm, in_sem.at[5])
     mixed_out.start()
-
-    relay_a.wait_recv()
-    add_slabs(xrel.at[0], a.at[right, 0], xrel.at[0])
-    last_a = remote(xrel.at[0], xin.at[0, 0], xs.at[4], xr.at[4], x=right)
-    relay_b.wait_recv()
-    add_slabs(xrel.at[1], a.at[left, 1], xrel.at[1])
-    last_b = remote(xrel.at[1], xin.at[1, 1], xs.at[5], xr.at[5], x=left)
-
-    for copy in (ynear_a, ynear_b, ylast_a, ylast_b):
-        copy.wait_recv()
-    add_slabs(b, wr.at[Y], yin.at[0], yin.at[1])
-
-    def slabs(x):
-        return b.at[span(x, 8)]
-
-    b_moved = [
-        remote(slabs(ring(X, d, 4)), xb.at[d], bs.at[d], br.at[d], x=ring(X, d, 4))
-        for d in (1, 3, 2)
-    ]
+    early = list(relays.values()) + to_core + list(w_halves.values())
+    early += list(halves.values())
+    for moved in (k_moved, v_moved, q_moved, g_moved, att_moved, dq_moved):
+        early += moved[0]
+    for pair in near.values():
+        early += pair
+    for copy in early:
+        copy.wait_send()
+    arrived(dq_moved)
 
     def give(t, src, dst):
         sent = [
@@ -327,22 +401,34 @@
         own.start()
         return sent, own
 
-    near_b.wait_recv()
-    last_a.wait_recv()
-    add_slabs(fin.at[0], a.at[X, 0], xin.at[0, 0], xin.at[1, 0])
-    dk_moved = give(6, fin.at[0], dko_ref)
-    near_a.wait_recv()
-    last_b.wait_recv()
-    add_slabs(fin.at[1], a.at[X, 1], xin.at[0, 1], xin.at[1, 1])
-    dv_moved = give(7, fin.at[1], dvo_ref)
-
-    for copy in b_moved:
-        copy.wait_recv()
-    add_slabs(c1, slabs(X), xb.at[1], xb.at[2], xb.at[3])
+    def settle(t, dst):
+        for name in ("near_a", "near_b", "last_a", "last_b"):
+            xmoves[name, t].wait_recv()
+        add_slabs(fin.at[t], a.at[X, t], xin.at[0, t], xin.at[1, t])
+        return give(6 + t, fin.at[t], dst)
+
+    dk_moved = settle(0, dko_ref)
+    weight_rows(1)
+
+    for h in range(2):
+        for d in (1, 3, 2):
+            b_moved[h, d].wait_recv()
+
+    @pl.loop(0, 8)
+    def _(z):
+        for h in range(2):
+            total = b[h, X * 8 + z].astype(F32)
+            for d in (1, 3, 2):
+                total += xb[h, d, z].astype(F32)
+            c1[z, :, h * 256 : h * 256 + 256] = total.astype(BF)
+
     c_moved = [
         remote(c1.at[ring(Z, d, 8)], zb.at[d], vs.at[d], vr.at[d], z=ring(Z, d, 8))
         for d in DISTANCES
     ]
+    dv_moved = settle(1, dvo_ref)
+    for copy in list(xmoves.values()) + list(ymoves.values()) + dk_moved[0]:
+        copy.wait_send()
     for copy in c_moved:
         copy.wait_recv()
     total = c1[Z].astype(F32)
@@ -355,20 +441,14 @@
         remote(wf, wout_ref.at[:, cols(Y, 512)], us.at[d], ur.at[d], rep=ring(Y, d, 4))
         for d in (1, 3, 2)
     ]
-    arrived(dq_moved)
     arrived(dk_moved)
     arrived(dv_moved)
     for copy in u_moved:
         copy.wait_recv()
     w_own.wait()
     mixed_out.wait()
-    sends = []
-    for moved in (k_moved, v_moved, q_moved, g_moved, att_moved, dq_moved, dk_moved, dv_moved):
-        sends += moved[0]
-    sends += to_right + to_left + to_core + relays + w_halves + halves
-    sends += [relay_a, relay_b, near_a, near_b, last_a, last_b]
-    sends += [yrelay_a, yrelay_b, ynear_a, ynear_b, ylast_a, ylast_b]
-    for copy in sends + b_moved + c_moved + u_moved:
+    late = dv_moved[0] + list(b_moved.values()) + c_moved + u_moved
+    for copy in late:
         copy.wait_send()
 
 
@@ -410,34 +490,37 @@
             vm((4, 2, 8, 128, HD), BF),
             vm((4, 2, 8, 128, HD), BF),
             vm((2, 2, 8, 128, HD), BF),
+            vm((2, 2, 4, 128, HD), BF),
             vm((2, 8, 128, HD), BF),
-            vm((2, 8, 128, HD), BF),
-            vm((2, 4, 32, 16, 512), BF),
-            vm((4, 32, 16, 512), BF),
-            vm((2, 16, 16, 512), BF),
-            vm((2, 32, 16, 512), BF),
-            vm((32, 16, 512), BF),
-            vm((4, 8, 16, 512), BF),
+            vm((2, 2, 4, 32, 16, 256), BF),
+            vm((2, 4, 32, 16, 256), BF),
+            vm((2, 2, 16, 16, 256), BF),
+            vm((2, 2, 32, 16, 256), BF),
+            vm((2, 32, 16, 256), BF),
+            vm((2, 4, 8, 16, 256), BF),
             vm((8, 16, 512), BF),
             vm((8, 16, 512), BF),
             vm((16, 512), F32),
             vm((128, 2048), BF),
+            vm((1024, 128), BF),
             dma((7,)),
             dma((8,)),
             dma((8, 8)),
             dma((8, 8)),
-            dma((2, 8)),
-            dma((2, 8)),
-            dma((4,)),
-            dma((4,)),
-            dma((6,)),
-            dma((6,)),
-            dma((4,)),
-            dma((4,)),
-            dma((6,)),
-            dma((6,)),
-            dma((4,)),
-            dma((4,)),
+            dma((2, 8, 3)),
+            dma((2, 8, 3)),
+            dma((2, 11)),
+            dma((2, 11)),
+            dma((2, 4)),
+            dma((2, 4)),
+            dma((2, 6)),
+            dma((2, 6)),
+            dma((2, 4)),
+            dma((2, 4)),
+            dma((2, 6)),
+            dma((2, 6)),
+            dma((2, 4)),
+            dma((2, 4)),
             dma((8,)),
             dma((8,)),
             dma((4,)),

time: 111 us -> 98.2 us (0.88)
  Pallas kernels: 105 us -> 93.5 us
    pallas_call x1, Pallas kernels: 103 us -> 91.2 us  [layer(): pl.pallas_call(layer_kernel, out_shape=OUTPUTS, in_specs=[pl.BlockSpec(me...]
where the time goes in v3:
time: 98.2 us; the launch traced here: 97.2 us
  Pallas kernels  93.5 us (95%)
  local copies, waits for them, and re-layouts  2.21 us (2%)
    pallas_call x1, Pallas kernels, layer(): pl.pallas_call(layer_kernel, out_shape=OUTPUTS, in_specs=[pl.BlockSpec(me...  91.2 us
    pallas_call x1, Pallas kernels, finish(): pl.pallas_call(finish_kernel, out_shape=OUTPUTS, in_specs=[anywhere] * 5,...  2.22 us

profile of v3, /device:TPU:2, one launch (start us, length us, event | category | flops | bytes accessed | tf_op | source)
XLA Modules:
  0.0 97.2 jit_solution(17157501207670535357)
XLA Ops:
  0.6 0.8 copy.12
  1.4 0.1 reshape.287
  1.5 0.5 broadcast.284
  2.0 0.7 fusion.8
  2.7 0.1 reshape_reshape.3
  2.8 0.1 eq.14
  2.9 0.2 select_reduce_fusion.1
  3.1 0.6 pad_add_fusion.tbl
  3.7 91.2 %layer.1 = (bf16[128,2048]{1,0:T(8,128)(2,1)}, bf16[128,1024]{1,0:T(8,128)(2,1)}, bf16[128,1024]{1,0:T(8,128)(2,1)}, bf16[128,1024]{1,0:T(8,128)(2,1)}, f32[16,2048]{1,0:T(8,128)}) custom-call(s32[3,128]{1,0:T(4,128)} %pad_add_fusion.tbl, bf16[2,64,1024]{2,1,0:T(8,128)(2,1)} %bitcast.14, bf16[2,64,1024]{2,1,0:T(8,128)(2,1)} %bitcast.15, ...), custom_call_target="tpu_custom_call" | custom-call | tf_op jit(solution)/shard_map/layer/pallas_call | solution.py:468
  95.0 2.2 %finish.1 = (bf16[128,2048]{1,0:T(8,128)(2,1)}, bf16[128,1024]{1,0:T(8,128)(2,1)}, bf16[128,1024]{1,0:T(8,128)(2,1)}, bf16[128,1024]{1,0:T(8,128)(2,1)}, f32[16,2048]{1,0:T(8,128)}) custom-call(bf16[128,2048]{1,0:T(8,128)(2,1)} %get-tuple-element.15.refs_0_, bf16[128,1024]{1,0:T(8,128)(2,1)} %get-tuple-element.16.refs_1_, ...), custom_call_target="tpu_custom_call" | custom-call | tf_op jit(solution)/shard_map/finish/pallas_call | solution.py:557
  (3 shorter events, 0.1 us)

commit v4 on v3

--- a/solution.py
+++ b/solution.py
@@ -69,8 +69,8 @@
     tbl, q_hbm, k_hbm, v_hbm, grad_hbm, weight_hbm,
     mixed_hbm, dqo_ref, dko_ref, dvo_ref, wout_ref,
     q_in, k_in, v_in, grad, weight, ag, kv, qs, gs, probs, o, dq, att, segk, segv,
-    given, r, a, xin, xrel, fin, wg, wr, yrel, yin, b, xb, c1, zb, wf, mixed, turned,
-    in_sem, own_sem, zs, zr, fs, fr, cs, cr, ks, kr, xs, xr, ws, wrs, ys, yr, bs, br, vs, vr, us, ur,
+    given, r, a, xin, xrel, fin, wg, wr, yrel, yin, b, xb, c1, zb, wf, mixed, turned, wall,
+    in_sem, own_sem, sent, one, zr, fr, kr, xr, wrs, yr,
 ):
     X, Z, C, Y = (lax.axis_index(n) for n in ("x", "z", "c", "rep"))
     loads = [
@@ -89,6 +89,10 @@
         + [{"rep": up}, {"rep": down}, {"rep": far}]
     )
 
+    def drain(sem, blocks):
+        whole = kv.at[pl.ds(0, blocks)]
+        pltpu.make_async_copy(whole, whole, sem).wait()
+
     def piece(c, x, t, first=0, count=8):
         return kv.at[pl.ds((((c * 4 + x) * 2 + t) * 8 + first) * 2, count * 2)]
 
@@ -100,21 +104,21 @@
     )
 
     def spread(t, src):
-        sent = [
+        arriving = [
             remote(
-                src.at[:, :, cols(ring(Z, d, 8))], targets[t](), zs.at[t, d], zr.at[t, d],
+                src.at[:, :, cols(ring(Z, d, 8))], targets[t](), sent.at[0],
+                zr.at[t, d - 1] if t < 2 else one.at[t],
                 z=ring(Z, d, 8),
             )
             for d in DISTANCES
         ]
         own = pltpu.make_async_copy(src.at[:, :, cols(Z)], targets[t](), own_sem.at[t])
         own.start()
-        return sent, own
-
-    def arrived(moved):
-        moved[1].wait()
-        for copy in moved[0]:
-            copy.wait_recv()
+        return arriving, own
+
+    def arrived(t, own):
+        own.wait()
+        drain(one.at[t], 14)
 
     loads[0].wait()
     k_moved = spread(0, k_in)
@@ -131,7 +135,7 @@
     ag[1] = rows[64:]
     g_moved = spread(3, ag)
 
-    near, relays, to_core = {}, {}, []
+    near, relays = {}, {}
 
     def send_near(t, d):
         if d == 0:
@@ -140,8 +144,8 @@
             moves[t][0][DISTANCES.index(d)].wait_recv()
         here = piece(C, X, t, ring(Z, -d, 8), 1)
         near[t, d] = (
-            remote(here, here, fs.at[t, d, 0], fr.at[t, d, 0], x=right),
-            remote(here, here, fs.at[t, d, 1], fr.at[t, d, 1], x=left),
+            remote(here, here, sent.at[0], fr.at[t, d, 0], x=right),
+            remote(here, here, sent.at[0], fr.at[t, d, 1], x=left),
         )
 
     def send_relay(t, d):
@@ -149,11 +153,11 @@
             copy.wait_recv()
         source, target = (left, right) if d < 4 else (right, left)
         here = piece(C, source, t, ring(Z, -d, 8), 1)
-        relays[t, d] = remote(here, here, fs.at[t, d, 2], fr.at[t, d, 2], x=target)
+        relays[t, d] = remote(here, here, sent.at[0], fr.at[t, d, 2], x=target)
 
     def across_core(t, n, x):
         here = piece(C, x, t)
-        to_core.append(remote(here, here, cs.at[t, n], cr.at[t, n], c=other))
+        remote(here, here, sent.at[1], one.at[0], c=other)
 
     moves = (k_moved, v_moved)
     steps = [(t, d) for t in range(2) for d in ARRIVALS]
@@ -171,15 +175,14 @@
         for d in ARRIVALS:
             relays[t, d].wait_recv()
             here = piece(C, across, t, ring(Z, -d, 8), 1)
-            to_core.append(remote(here, here, cs.at[t, 3 + d], cr.at[t, 3 + d], c=other))
-    arrived(q_moved)
-    for copy in to_core:
-        copy.wait_recv()
-
-    def gathered(i, extra):
+            remote(here, here, sent.at[1], one.at[0], c=other)
+    arrived(2, q_moved[1])
+    drain(one.at[0], 128)
+
+    def gathered(m, extra):
         return jnp.concatenate(
             [
-                kv[tbl[0, i * 8 + j] + extra]
+                kv[tbl[0, j * 16 + m] + extra]
                 for j in range(8)
             ],
             axis=0,
@@ -188,21 +191,21 @@
     def out_copy(t, n, src, dst):
         z = lax.rem(Z + n + 1, 8)
         return link(
-            src.at[span(z, 128)], dst.at[:, cols(Z)], zs.at[t, n + 1], zr.at[t, n + 1], z=z
+            src.at[span(z, 128)], dst.at[:, cols(Z)], sent.at[2], one.at[t], z=z
         )
 
     @pl.loop(0, 8)
     def _(n):
         z = lax.rem(Z + n + 1, 8)
         for half in range(2):
-            i = z * 2 + half
+            i, m = z * 2 + half, n * 2 + half
             rows = span(i, 64)
-            s = lax.dot_general(qs[i], gathered(i, 0), NT, preferred_element_type=F32) * SCALE
+            s = lax.dot_general(qs[i], gathered(m, 0), NT, preferred_element_type=F32) * SCALE
             e = jnp.exp(s - jnp.max(s, axis=-1, keepdims=True))
             p = e / jnp.sum(e, axis=-1, keepdims=True)
             probs[rows, :] = p
             o[rows, :] = jnp.dot(
-                p.astype(BF), gathered(i, 16), preferred_element_type=F32
+                p.astype(BF), gathered(m, 16), preferred_element_type=F32
             ).astype(BF)
 
         @pl.when(n < 7)
@@ -211,19 +214,18 @@
 
     att_own = pltpu.make_async_copy(o.at[span(Z, 128)], att.at[:, cols(Z)], own_sem.at[4])
     att_own.start()
-    att_moved = [out_copy(4, n, o, att) for n in range(7)], att_own
-    arrived(g_moved)
+    arrived(3, g_moved[1])
 
     def backward(first, last):
         @pl.loop(first, last)
         def _(n):
             z = lax.rem(Z + n + 1, 8)
             for half in range(2):
-                i = z * 2 + half
+                i, m = z * 2 + half, n * 2 + half
                 rows = span(i, 64)
                 q, g, p = qs[i], gs[i], probs[rows, :]
-                kg = gathered(i, 0)
-                dp = lax.dot_general(g, gathered(i, 16), NT, preferred_element_type=F32)
+                kg = gathered(m, 0)
+                dp = lax.dot_general(g, gathered(m, 16), NT, preferred_element_type=F32)
                 delta = jnp.sum(p * dp, axis=-1, keepdims=True)
                 ds = (p * (dp - delta)).astype(BF)
                 dq[rows, :] = (
@@ -231,11 +233,10 @@
                 ).astype(BF)
                 dk = lax.dot_general(ds, q, TN, preferred_element_type=F32)
                 dv = lax.dot_general(p.astype(BF), g, TN, preferred_element_type=F32)
-                m = n * 2 + half
                 for j in range(8):
-                    before = tbl[1, m * 8 + j]
-                    segk[m * 8 + j] = segk[before] + dk[j * 64 : j * 64 + 64]
-                    segv[m * 8 + j] = segv[before] + dv[j * 64 : j * 64 + 64]
+                    before = tbl[1, j * 16 + m]
+                    segk[j * 16 + m] = segk[before] + dk[j * 64 : j * 64 + 64]
+                    segv[j * 16 + m] = segv[before] + dv[j * 64 : j * 64 + 64]
 
             @pl.when(n < 7)
             def _():
@@ -244,8 +245,7 @@
     backward(0, 8)
     dq_own = pltpu.make_async_copy(dq.at[span(Z, 128)], dqo_ref.at[:, cols(Z)], own_sem.at[5])
     dq_own.start()
-    dq_moved = [out_copy(5, n, dq, dqo_ref) for n in range(7)], dq_own
-    arrived(att_moved)
+    arrived(4, att_own)
 
     def collect(x, core, t, dst, more=None):
         @pl.loop(0, 8)
@@ -272,13 +272,13 @@
                 wg[h, k % 2, y, m * 8 + k // 2] = rows[k * 16 : k * 16 + 16]
 
         w_halves[h, n] = remote(
-            wg.at[h, other, y], wr.at[h, y], ws.at[h, n], wrs.at[h, n], c=other
+            wg.at[h, other, y], wr.at[h, y], sent.at[2], wrs.at[h, n], c=other
         )
 
     def share_keys(t):
         for n, x in enumerate((across, right, left, X)):
             collect(x, other, t, given.at[x, t])
-            halves[t, n] = remote(given.at[x, t], r.at[x, t], ks.at[t, n], kr.at[t, n], c=other)
+            halves[t, n] = remote(given.at[x, t], r.at[x, t], sent.at[3], kr.at[t, n], c=other)
 
     def take(t, n, x):
         halves[t, n].wait_recv()
@@ -288,7 +288,7 @@
     xmoves = {}
 
     def xsend(name, t, n, src, dst, target):
-        xmoves[name, t] = remote(src, dst, xs.at[t, n], xr.at[t, n], x=target)
+        xmoves[name, t] = remote(src, dst, sent.at[4], xr.at[t, n], x=target)
 
     def chunk_across(t):
         take(t, 0, across)
@@ -308,7 +308,7 @@
     low, high = pl.ds(0, 16), pl.ds(16, 16)
 
     def ysend(name, h, n, src, dst, target):
-        ymoves[name, h] = remote(src, dst, ys.at[h, n], yr.at[h, n], rep=target)
+        ymoves[name, h] = remote(src, dst, sent.at[4], yr.at[h, n], rep=target)
 
     def weight_far(h):
         weight_chunk(h, 0, far)
@@ -329,8 +329,6 @@
         add_slabs(yrel.at[h, 1], wr.at[h, down, high], yrel.at[h, 1])
         ysend("last_b", h, 5, yrel.at[h, 1], yin.at[h, 1, high], down)
 
-    b_moved = {}
-
     def slabs(h, x):
         return b.at[h, span(x, 8)]
 
@@ -339,8 +337,8 @@
             ymoves[name, h].wait_recv()
         add_slabs(b.at[h], wr.at[h, Y], yin.at[h, 0], yin.at[h, 1])
         for d in (1, 3, 2):
-            b_moved[h, d] = remote(
-                slabs(h, ring(X, d, 4)), xb.at[h, d], bs.at[h, d], br.at[h, d], x=ring(X, d, 4)
+            remote(
+                slabs(h, ring(X, d, 4)), xb.at[h, d], sent.at[5], one.at[1], x=ring(X, d, 4)
             )
 
     def xpass(t):
@@ -381,38 +379,31 @@
     mixed[...] = jnp.dot(att[...], weight[...], preferred_element_type=F32).astype(BF)
     mixed_out = pltpu.make_async_copy(mixed, mixed_hbm, in_sem.at[5])
     mixed_out.start()
-    early = list(relays.values()) + to_core + list(w_halves.values())
-    early += list(halves.values())
-    for moved in (k_moved, v_moved, q_moved, g_moved, att_moved, dq_moved):
-        early += moved[0]
-    for pair in near.values():
-        early += pair
-    for copy in early:
-        copy.wait_send()
-    arrived(dq_moved)
-
-    def give(t, src, dst):
-        sent = [
-            remote(src.at[ring(Z, d, 8)], dst.at[:, cols(Z)], zs.at[t, d], zr.at[t, d],
-                   z=ring(Z, d, 8))
-            for d in DISTANCES
-        ]
-        own = pltpu.make_async_copy(src.at[Z], dst.at[:, cols(Z)], own_sem.at[t])
-        own.start()
-        return sent, own
-
-    def settle(t, dst):
+    for n, blocks in enumerate((152, 128, 156, 128)):
+        drain(sent.at[n], blocks)
+    arrived(5, dq_own)
+
+    def give(t, src, dst, distances):
+        for d in distances:
+            remote(
+                src.at[ring(Z, d, 8)], dst.at[:, cols(Z)], sent.at[5], one.at[t],
+                z=ring(Z, d, 8),
+            )
+
+    def settle(t, dst, distances):
         for name in ("near_a", "near_b", "last_a", "last_b"):
             xmoves[name, t].wait_recv()
         add_slabs(fin.at[t], a.at[X, t], xin.at[0, t], xin.at[1, t])
-        return give(6 + t, fin.at[t], dst)
-
-    dk_moved = settle(0, dko_ref)
+        own = pltpu.make_async_copy(fin.at[t, Z], dst.at[:, cols(Z)], own_sem.at[6 + t])
+        own.start()
+        give(6 + t, fin.at[t], dst, distances)
+        return own
+
+    dk_own = settle(0, dko_ref, DISTANCES)
     weight_rows(1)
-
-    for h in range(2):
-        for d in (1, 3, 2):
-            b_moved[h, d].wait_recv()
+    dv_own = settle(1, dvo_ref, (4, 3, 5, 2))
+
+    drain(one.at[1], 24)
 
     @pl.loop(0, 8)
     def _(z):
@@ -422,34 +413,26 @@
                 total += xb[h, d, z].astype(F32)
             c1[z, :, h * 256 : h * 256 + 256] = total.astype(BF)
 
-    c_moved = [
-        remote(c1.at[ring(Z, d, 8)], zb.at[d], vs.at[d], vr.at[d], z=ring(Z, d, 8))
-        for d in DISTANCES
-    ]
-    dv_moved = settle(1, dvo_ref)
-    for copy in list(xmoves.values()) + list(ymoves.values()) + dk_moved[0]:
-        copy.wait_send()
-    for copy in c_moved:
-        copy.wait_recv()
+    for d in DISTANCES:
+        remote(c1.at[ring(Z, d, 8)], zb.at[d], sent.at[5], one.at[8], z=ring(Z, d, 8))
+    give(7, fin.at[1], dvo_ref, (6, 1, 7))
+    drain(sent.at[4], 192)
+    drain(one.at[8], 7)
     total = c1[Z].astype(F32)
     for d in DISTANCES:
         total += zb[d].astype(F32)
     wf[...] = total * (1.0 / math.sqrt(32768))
-    w_own = pltpu.make_async_copy(wf, wout_ref.at[:, cols(Y, 512)], in_sem.at[6])
+    wall[:, cols(Y, 512)] = wf[...]
+    for d in (1, 3, 2):
+        remote(wf, wall.at[:, cols(Y, 512)], sent.at[5], one.at[9], rep=ring(Y, d, 4))
+    drain(one.at[9], 6)
+    w_own = pltpu.make_async_copy(wall, wout_ref, in_sem.at[6])
     w_own.start()
-    u_moved = [
-        remote(wf, wout_ref.at[:, cols(Y, 512)], us.at[d], ur.at[d], rep=ring(Y, d, 4))
-        for d in (1, 3, 2)
-    ]
-    arrived(dk_moved)
-    arrived(dv_moved)
-    for copy in u_moved:
-        copy.wait_recv()
+    arrived(6, dk_own)
+    arrived(7, dv_own)
+    mixed_out.wait()
+    drain(sent.at[5], 65)
     w_own.wait()
-    mixed_out.wait()
-    late = dv_moved[0] + list(b_moved.values()) + c_moved + u_moved
-    for copy in late:
-        copy.wait_send()
 
 
 OUTPUTS = (
@@ -503,28 +486,17 @@
             vm((16, 512), F32),
             vm((128, 2048), BF),
             vm((1024, 128), BF),
+            vm((16, 2048), F32),
             dma((7,)),
             dma((8,)),
-            dma((8, 8)),
-            dma((8, 8)),
+            dma((6,)),
+            dma((10,)),
+            dma((2, 7)),
             dma((2, 8, 3)),
-            dma((2, 8, 3)),
-            dma((2, 11)),
-            dma((2, 11)),
-            dma((2, 4)),
             dma((2, 4)),
             dma((2, 6)),
-            dma((2, 6)),
-            dma((2, 4)),
             dma((2, 4)),
             dma((2, 6)),
-            dma((2, 6)),
-            dma((2, 4)),
-            dma((2, 4)),
-            dma((8,)),
-            dma((8,)),
-            dma((4,)),
-            dma((4,)),
         ],
         compiler_params=pltpu.CompilerParams(
             collective_id=0, has_side_effects=True, vmem_limit_bytes=63 << 20
@@ -568,21 +540,21 @@
 
 def tables_of(pattern):
     X, Z, C = (lax.axis_index(n) for n in "xzc")
-    by_owner = pattern.reshape(4, 8, 2, 16)
-    mine = lax.dynamic_slice(by_owner, (X, 0, C, 0), (1, 8, 1, 16)).reshape(8, 16)
-    plain = mine.reshape(128)
-    turned = jnp.concatenate([mine, mine], axis=0)
-    turned = lax.dynamic_slice(turned, (lax.rem(Z + 1, 8), 0), (8, 16)).reshape(128)
-    s = plain // 2
-    places = ((s % 2) * 4 + s // 16) * 32 + ((s // 2) % 8) * 2 + plain % 2
-    order = jnp.arange(128, dtype=jnp.int32)
-    same = turned[None, :] == turned[:, None]
+    m = jnp.arange(16, dtype=jnp.int32)
+    t = jnp.arange(128, dtype=jnp.int32)
+    rows = X * 32 + ((Z + 1 + (m >> 1)) & 7) * 4 + C * 2 + (m & 1)
+    chosen = rows[None, :, None] == t[None, None, :]
+    mine = jnp.sum(jnp.where(chosen, pattern.T[:, None, :], 0), axis=2).reshape(128)
+    s = mine >> 1
+    places = ((s & 1) * 4 + (s >> 4)) * 32 + ((s >> 1) & 7) * 2 + (mine & 1)
+    order = (t & 15) * 8 + (t >> 4)
+    same = mine[None, :] == mine[:, None]
     earlier = order[None, :] < order[:, None]
     before = jnp.max(jnp.where(same & earlier, order[None, :], -1), axis=1)
-    last = jnp.max(jnp.where(turned[None, :] == order[:, None], order[None, :], -1), axis=1)
-    return jnp.stack(
-        [places, jnp.where(before < 0, 128, before), jnp.where(last < 0, 128, last)]
-    )
+    last = jnp.max(jnp.where(mine[None, :] == t[:, None], order[None, :], -1), axis=1)
+    links = jnp.stack([before, last])
+    links = jnp.where(links < 0, 128, (links & 7) * 16 + (links >> 3))
+    return jnp.concatenate([places[None], links])
 
 
 def local(query_in, key_in, value_in, out_weight, grad_out, pattern):

time: 98.2 us -> 95.2 us (0.969)
  local copies, waits for them, and re-layouts: 2.21 us -> 0.16 us
  Pallas kernels: 93.5 us -> 92.4 us
    dynamic_slice x2 -> x0, local copies, waits for them, and re-layouts: 1.18 us -> none  [tables_of(): lax.dynamic_slice(by_owner, (X, 0, C, 0), (1, 8, 1, 16)).reshape(8, 16)]
    pallas_call x1, Pallas kernels: 91.2 us -> 90.2 us  [layer(): pl.pallas_call(layer_kernel, out_shape=OUTPUTS, in_specs=[pl.BlockSpec(me...]
where the time goes in v4:
time: 95.2 us; the launch traced here: 95.1 us
  Pallas kernels  92.4 us (97%)
  other arithmetic  1.79 us (2%)
    pallas_call x1, Pallas kernels, layer(): pl.pallas_call(layer_kernel, out_shape=OUTPUTS, in_specs=[pl.BlockSpec(me...  90.2 us
    pallas_call x1, Pallas kernels, finish(): pl.pallas_call(finish_kernel, out_shape=OUTPUTS, in_specs=[anywhere] * 5,...  2.22 us

profile of v4, /device:TPU:2, one launch (start us, length us, event | category | flops | bytes accessed | tf_op | source)
XLA Modules:
  0.0 95.1 jit_solution(3420500700792330426)
XLA Ops:
  0.7 0.1 iota_compare_fusion.1
  0.7 0.9 select_reduce_fusion.2
  1.6 0.1 eq.47
  1.7 0.1 reshape.146
  1.8 0.2 select_reduce_fusion.1
  2.0 0.6 pad_add_fusion.tbl
  2.6 90.2 %layer.1 = (bf16[128,2048]{1,0:T(8,128)(2,1)}, bf16[128,1024]{1,0:T(8,128)(2,1)}, bf16[128,1024]{1,0:T(8,128)(2,1)}, bf16[128,1024]{1,0:T(8,128)(2,1)}, f32[16,2048]{1,0:T(8,128)}) custom-call(s32[3,128]{1,0:T(4,128)} %pad_add_fusion.tbl, bf16[2,64,1024]{2,1,0:T(8,128)(2,1)} %bitcast.12, bf16[2,64,1024]{2,1,0:T(8,128)(2,1)} %bitcast.13, ...), custom_call_target="tpu_custom_call" | custom-call | tf_op jit(solution)/shard_map/layer/pallas_call | solution.py:451
  92.8 2.2 %finish.1 = (bf16[128,2048]{1,0:T(8,128)(2,1)}, bf16[128,1024]{1,0:T(8,128)(2,1)}, bf16[128,1024]{1,0:T(8,128)(2,1)}, bf16[128,1024]{1,0:T(8,128)(2,1)}, f32[16,2048]{1,0:T(8,128)}) custom-call(bf16[128,2048]{1,0:T(8,128)(2,1)} %get-tuple-element.15.refs_0_, bf16[128,1024]{1,0:T(8,128)(2,1)} %get-tuple-element.16.refs_1_, ...), custom_call_target="tpu_custom_call" | custom-call | tf_op jit(solution)/shard_map/finish/pallas_call | solution.py:529
  (4 shorter events, 0.0 us)

commit v5 on v4

--- a/solution.py
+++ b/solution.py
@@ -161,14 +161,14 @@
 
     moves = (k_moved, v_moved)
     steps = [(t, d) for t in range(2) for d in ARRIVALS]
-    for n in range(len(steps) + 4):
+    for n in range(len(steps) + 6):
         if n < len(steps):
             send_near(*steps[n])
             if n % 8 == 7:
                 across_core(n // 8, 0, X)
-        if n >= 4:
-            send_relay(*steps[n - 4])
-            if n % 8 == 3:
+        if n >= 6:
+            send_relay(*steps[n - 6])
+            if n % 8 == 5:
                 across_core(n // 8 - 1, 1, left)
                 across_core(n // 8 - 1, 2, right)
     for t in range(2):

time: 95.2 us -> 94.8 us (level)
  Pallas kernels: 92.4 us -> 91.1 us
    pallas_call x1, Pallas kernels: 90.2 us -> 88.9 us  [layer(): pl.pallas_call(layer_kernel, out_shape=OUTPUTS, in_specs=[pl.BlockSpec(me...]
where the time goes in v5:
time: 94.8 us; the launch traced here: 93.7 us
  Pallas kernels  91.1 us (96%)
  other arithmetic  1.79 us (2%)
    pallas_call x1, Pallas kernels, layer(): pl.pallas_call(layer_kernel, out_shape=OUTPUTS, in_specs=[pl.BlockSpec(me...  88.9 us
    pallas_call x1, Pallas kernels, finish(): pl.pallas_call(finish_kernel, out_shape=OUTPUTS, in_specs=[anywhere] * 5,...  2.22 us

profile of v5, /device:TPU:2, one launch (start us, length us, event | category | flops | bytes accessed | tf_op | source)
XLA Modules:
  0.0 93.7 jit_solution(101315620843611477)
XLA Ops:
  0.7 0.1 iota_compare_fusion.1
  0.7 0.9 select_reduce_fusion.2
  1.6 0.1 eq.47
  1.7 0.1 reshape.146
  1.8 0.2 select_reduce_fusion.1
  2.0 0.6 pad_add_fusion.tbl
  2.6 88.9 %layer.1 = (bf16[128,2048]{1,0:T(8,128)(2,1)}, bf16[128,1024]{1,0:T(8,128)(2,1)}, bf16[128,1024]{1,0:T(8,128)(2,1)}, bf16[128,1024]{1,0:T(8,128)(2,1)}, f32[16,2048]{1,0:T(8,128)}) custom-call(s32[3,128]{1,0:T(4,128)} %pad_add_fusion.tbl, bf16[2,64,1024]{2,1,0:T(8,128)(2,1)} %bitcast.12, bf16[2,64,1024]{2,1,0:T(8,128)(2,1)} %bitcast.13, ...), custom_call_target="tpu_custom_call" | custom-call | tf_op jit(solution)/shard_map/layer/pallas_call | solution.py:451
  91.5 2.2 %finish.1 = (bf16[128,2048]{1,0:T(8,128)(2,1)}, bf16[128,1024]{1,0:T(8,128)(2,1)}, bf16[128,1024]{1,0:T(8,128)(2,1)}, bf16[128,1024]{1,0:T(8,128)(2,1)}, f32[16,2048]{1,0:T(8,128)}) custom-call(bf16[128,2048]{1,0:T(8,128)(2,1)} %get-tuple-element.15.refs_0_, bf16[128,1024]{1,0:T(8,128)(2,1)} %get-tuple-element.16.refs_1_, ...), custom_call_target="tpu_custom_call" | custom-call | tf_op jit(solution)/shard_map/finish/pallas_call | solution.py:529
  (4 shorter events, 0.0 us)
